TPU v7x, 256 devices: a whole 4x4x8 slice. The times are simulated.
256 devices in a mesh: dp: 8 (over y, core), expert: 32 (over x, z).
Axes of the slice: x: 4, y: 4, z: 8, core: 2. Of those that a mesh axis runs over, the one named last changes fastest.
Arguments:
- tokens: bfloat16 [2048, 3584], P(('dp', 'expert')), may hold values from -6 to 6
- routes: int32 [2048, 8], P(('dp', 'expert')), may hold values from 0 to 63, all different within a row; in each aligned block of 8 rows (0 to 7, 8 to 15, ...) at most 2 rows name the same one
- gates: bfloat16 [2048, 8], P(('dp', 'expert')), may hold values from 0.049804688 to 0.5
- cotangent: bfloat16 [2048, 3584], P(('dp', 'expert')), may hold values from -1.5 to 1.5
- w_gate: bfloat16 [64, 3584, 1024], P('expert', None, 'dp'), may hold values from -0.09375 to 0.09375
- w_up: bfloat16 [64, 3584, 1024], P('expert', None, 'dp'), may hold values from -0.09375 to 0.09375
- w_down: bfloat16 [64, 1024, 3584], P('expert', 'dp'), may hold values from -0.1875 to 0.1875
Outputs:
- token_grads: bfloat16 [2048, 3584], P(('dp', 'expert'))
- gate_grads: float32 [2048, 8], P(('dp', 'expert'))
- grad_gate: bfloat16 [64, 3584, 1024], P('expert', None, 'dp')
- grad_up: bfloat16 [64, 3584, 1024], P('expert', None, 'dp')
- grad_down: bfloat16 [64, 1024, 3584], P('expert', 'dp')
Inputs may be any that keep to these rules, and one draw needn't show every extreme that they name: `routes`: each row names 8 different experts. Within each device's block of 8 rows no expert is named by more than 2 rows, a bound that some block reaches.
All inputs are finite; a program needn't handle non-finite values.
Results may differ from a plain program's by a relative error of at most 0.0058.
Values may be sent and summed in bfloat16 or wider, within the bound.
A program may use at most 192 MiB of HBM per device.

v0:
```python
from functools import partial

import jax
import jax.numpy as jnp
from jax import lax
from jax.sharding import PartitionSpec as P

TOPK = 8


def route_table(routes, experts_all, capacity):
    pairs = routes.reshape(-1)
    onehot = (pairs[:, None] == jnp.arange(experts_all, dtype=jnp.int32)[None, :]).astype(jnp.int32)
    before = jnp.cumsum(onehot, axis=0) - onehot
    within = jnp.sum(before * onehot, axis=1)
    target = pairs * capacity + within
    slot_ids = jnp.arange(experts_all * capacity, dtype=jnp.int32)
    return (target[:, None] == slot_ids[None, :]).astype(jnp.float32)


def dispatch(table, tokens, cotangent, gates):
    count = tokens.shape[0]
    slots = table.shape[1]
    spread = table.reshape(count, TOPK, slots).sum(axis=1).astype(jnp.bfloat16)
    slot_tokens = jnp.einsum(
        "ts,td->sd", spread, tokens, preferred_element_type=jnp.float32
    ).astype(jnp.bfloat16)
    slot_cot = jnp.einsum(
        "ts,td->sd", spread, cotangent, preferred_element_type=jnp.float32
    ).astype(jnp.bfloat16)
    flat_gates = gates.reshape(-1).astype(jnp.float32)
    slot_gates = jnp.einsum("ps,p->s", table, flat_gates, precision=lax.Precision.HIGHEST).astype(
        jnp.bfloat16
    )
    return (slot_tokens, slot_cot, slot_gates)


def expert_work(slot_tokens, slot_cot, slot_gates, w_gate, w_up, w_down):
    gate_pre = jnp.einsum("rjcd,jdh->rjch", slot_tokens, w_gate, preferred_element_type=jnp.float32)
    upper_pre = jnp.einsum("rjcd,jdh->rjch", slot_tokens, w_up, preferred_element_type=jnp.float32)
    gate_sig = jax.nn.sigmoid(gate_pre)
    active = (gate_pre * gate_sig * upper_pre).astype(jnp.bfloat16)
    output = jnp.einsum("rjch,jhd->rjcd", active, w_down, preferred_element_type=jnp.float32)
    cot_float = slot_cot.astype(jnp.float32)
    gate_part = jnp.sum(output * cot_float, axis=-1)
    scaled = (slot_gates.astype(jnp.float32)[..., None] * cot_float).astype(jnp.bfloat16)
    grad_active = jnp.einsum("rjcd,jhd->rjch", scaled, w_down, preferred_element_type=jnp.float32)
    grad_upper = (grad_active * gate_pre * gate_sig).astype(jnp.bfloat16)
    grad_gpre = (grad_active * upper_pre * gate_sig * (1.0 + gate_pre * (1.0 - gate_sig))).astype(
        jnp.bfloat16
    )
    token_part = jnp.einsum("rjch,jdh->rjcd", grad_gpre, w_gate, preferred_element_type=jnp.float32)
    token_part = token_part + jnp.einsum(
        "rjch,jdh->rjcd", grad_upper, w_up, preferred_element_type=jnp.float32
    )
    grad_g = jnp.einsum(
        "rjcd,rjch->jdh", slot_tokens, grad_gpre, preferred_element_type=jnp.float32
    ).astype(jnp.bfloat16)
    grad_u = jnp.einsum(
        "rjcd,rjch->jdh", slot_tokens, grad_upper, preferred_element_type=jnp.float32
    ).astype(jnp.bfloat16)
    grad_d = jnp.einsum(
        "rjch,rjcd->jhd", active, scaled, preferred_element_type=jnp.float32
    ).astype(jnp.bfloat16)
    return (token_part, gate_part, grad_g, grad_u, grad_d)


def local(tokens, routes, gates, cotangent, w_gate, w_up, w_down):
    n_expert = lax.axis_size("expert")
    n_groups = lax.axis_size("dp")
    local_experts = w_gate.shape[0]
    experts_all = local_experts * n_expert
    tok_count = tokens.shape[0]
    width = tokens.shape[1]
    capacity = 16 * tok_count // experts_all
    slots = experts_all * capacity
    make_table = partial(route_table, experts_all=experts_all, capacity=capacity)
    all_tokens, all_cot, all_gates = (
        lax.all_gather(tokens, "dp", axis=0, tiled=True),
        lax.all_gather(cotangent, "dp", axis=0, tiled=True),
        lax.all_gather(gates, "dp", axis=0, tiled=True),
    )
    all_routes = lax.all_gather(routes, "dp", axis=0, tiled=True)
    all_routes = all_routes.reshape(n_groups, tok_count, TOPK)
    tables = jax.vmap(make_table)(all_routes)
    slot_tokens, slot_cot, slot_gates = jax.vmap(dispatch)(
        tables,
        all_tokens.reshape(n_groups, tok_count, width),
        all_cot.reshape(n_groups, tok_count, width),
        all_gates.reshape(n_groups, tok_count, TOPK),
    )
    slot_tokens = slot_tokens.reshape(n_groups, n_expert, local_experts * capacity, width)
    slot_cot = slot_cot.reshape(n_groups, n_expert, local_experts * capacity, width)
    slot_gates = slot_gates.reshape(n_groups, n_expert, local_experts * capacity)
    recv_tokens, recv_cot, recv_gates = (
        lax.all_to_all(slot_tokens, "expert", split_axis=1, concat_axis=1, tiled=True),
        lax.all_to_all(slot_cot, "expert", split_axis=1, concat_axis=1, tiled=True),
        lax.all_to_all(slot_gates, "expert", split_axis=1, concat_axis=1, tiled=True),
    )
    rows = n_groups * n_expert
    token_part, gate_part, grad_gate, grad_up, grad_down = expert_work(
        recv_tokens.reshape(rows, local_experts, capacity, width),
        recv_cot.reshape(rows, local_experts, capacity, width),
        recv_gates.reshape(rows, local_experts, capacity),
        w_gate,
        w_up,
        w_down,
    )
    token_part = token_part.reshape(n_groups, n_expert, local_experts * capacity, width)
    gate_part = gate_part.reshape(n_groups, n_expert, local_experts * capacity)
    back_tokens, back_gates = (
        lax.all_to_all(token_part, "expert", split_axis=1, concat_axis=1, tiled=True),
        lax.all_to_all(gate_part, "expert", split_axis=1, concat_axis=1, tiled=True),
    )
    back_tokens = back_tokens.reshape(n_groups, slots, width)
    back_gates = back_gates.reshape(n_groups, slots)
    spread = tables.reshape(n_groups, tok_count, TOPK, slots).sum(axis=2)
    token_sum = jnp.einsum("gts,gsd->gtd", spread, back_tokens, precision=lax.Precision.HIGHEST)
    gate_sum = jnp.einsum("gps,gs->gp", tables, back_gates, precision=lax.Precision.HIGHEST)
    token_total, gate_total = (
        lax.psum_scatter(token_sum, "dp", scatter_dimension=0, tiled=True),
        lax.psum_scatter(gate_sum, "dp", scatter_dimension=0, tiled=True),
    )
    token_grads = token_total[0].astype(jnp.bfloat16)
    gate_grads = gate_total[0].reshape(tok_count, TOPK)
    return (token_grads, gate_grads, grad_gate, grad_up, grad_down)


def solution(mesh):
    return jax.shard_map(
        local,
        mesh=mesh,
        in_specs=(
            P(("dp", "expert"), None),
            P(("dp", "expert"), None),
            P(("dp", "expert"), None),
            P(("dp", "expert"), None),
            P("expert", None, "dp"),
            P("expert", None, "dp"),
            P("expert", "dp", None),
        ),
        out_specs=(
            P(("dp", "expert"), None),
            P(("dp", "expert"), None),
            P("expert", None, "dp"),
            P("expert", None, "dp"),
            P("expert", "dp", None),
        ),
        check_vma=False,
    )
```

profile of v0, /device:TPU:32, one launch (start us, length us, event | category | flops | bytes accessed | tf_op | source)
XLA Modules:
  0.0 934.7 jit_solution(15179347761495512398)
XLA Ops:
  7.2 12.5 %all_gather.13 = bf16[64,8]{1,0:T(8,128)(2,1)S(1)} all-gather(bf16[8,8]{1,0:T(8,128)(2,1)} %param.9), channel_id=1, replica_groups=mesh['dp'=8,'expert'=32] {'dp'}, dimensions={0}, use_global_device_ids=true | all-gather | bytes 1152 | tf_op jit(solution)/shard_map/all_gather | solution.py:81
  19.7 13.0 %all_gather.12 = s32[64,8]{1,0:T(8,128)S(1)} all-gather(s32[8,8]{1,0:T(8,128)} %param.8), channel_id=1, replica_groups=mesh['dp'=8,'expert'=32] {'dp'}, dimensions={0}, use_global_device_ids=true | all-gather | bytes 2304 | tf_op jit(solution)/shard_map/all_gather | solution.py:83
  35.4 11.2 %all-to-all-start = ((bf16[8,32,4]{0,2,1:T(4,128)(2,1)}), bf16[8,32,4]{0,2,1:T(4,128)(2,1)S(1)}, u32[]{:S(2)}, u32[]{:S(2)}) async-start(bf16[8,32,4]{0,2,1:T(4,128)(2,1)} %bitcast.3), calls=%async_computation | async-start | bytes 65536 | tf_op jit(solution)/shard_map/all_to_all | solution.py:98
  46.9 13.3 %all_gather.14 = bf16[64,3584]{1,0:T(8,128)(2,1)S(1)} all-gather(bf16[8,3584]{1,0:T(8,128)(2,1)} %param.10), channel_id=1, replica_groups=mesh['dp'=8,'expert'=32] {'dp'}, dimensions={0}, use_global_device_ids=true | all-gather | bytes 516096 | tf_op jit(solution)/shard_map/all_gather | solution.py:80
  60.2 5.1 convolution_convert_fusion.1
  65.3 12.6 %reshape.71 = bf16[8,32,4,3584]{3,2,1,0:T(4,128)(2,1)} reshape(bf16[8,128,3584]{2,1,0:T(8,128)(2,1)} %convolution_convert_fusion.1) | data formatting | bytes 14680064 | tf_op jit(solution)/shard_map/reshape | solution.py:93
  77.9 9.9 %copy.104 = bf16[8,32,4,3584]{3,2,0,1:T(4,128)(2,1)} copy(bf16[8,32,4,3584]{3,2,1,0:T(4,128)(2,1)} %reshape.71) | data formatting | bytes 14680064 | tf_op jit(solution)/shard_map/reshape | solution.py:93
  87.9 10.0 %all-to-all-start.1 = ((bf16[8,32,4,3584]{3,2,0,1:T(4,128)(2,1)}), bf16[8,32,4,3584]{3,2,0,1:T(4,128)(2,1)}, u32[]{:S(2)}, u32[]{:S(2)}) async-start(bf16[8,32,4,3584]{3,2,0,1:T(4,128)(2,1)} %copy.104), calls=%async_computation.1 | async-start | bytes 14680064 | tf_op jit(solution)/shard_map/all_to_all | solution.py:97
  97.8 13.3 %all_gather.15 = bf16[64,3584]{1,0:T(8,128)(2,1)S(1)} all-gather(bf16[8,3584]{1,0:T(8,128)(2,1)S(1)} %copy-done.9), channel_id=1, replica_groups=mesh['dp'=8,'expert'=32] {'dp'}, dimensions={0}, use_global_device_ids=true | all-gather | bytes 516096 | tf_op jit(solution)/shard_map/all_gather | solution.py:79
  111.1 5.1 convolution_convert_fusion
  116.2 12.7 %reshape.73 = bf16[8,32,4,3584]{3,2,1,0:T(4,128)(2,1)} reshape(bf16[8,128,3584]{2,1,0:T(8,128)(2,1)} %convolution_convert_fusion) | data formatting | bytes 14680064 | tf_op jit(solution)/shard_map/reshape | solution.py:92
  128.8 9.9 %copy.107 = bf16[8,32,4,3584]{3,2,0,1:T(4,128)(2,1)} copy(bf16[8,32,4,3584]{3,2,1,0:T(4,128)(2,1)} %reshape.73) | data formatting | bytes 14680064 | tf_op jit(solution)/shard_map/reshape | solution.py:92
  138.7 127.7 %all-to-all-done.1 = bf16[8,32,4,3584]{3,2,0,1:T(4,128)(2,1)} async-done(((bf16[8,32,4,3584]{3,2,0,1:T(4,128)(2,1)}), bf16[8,32,4,3584]{3,2,0,1:T(4,128)(2,1)}, u32[]{:S(2)}, u32[]{:S(2)}) %all-to-all-start.1) | async-done | bytes 7340064 | tf_op jit(solution)/shard_map/all_to_all | solution.py:97
  266.4 14.5 %all-to-all-start.2 = ((bf16[8,32,4,3584]{3,2,0,1:T(4,128)(2,1)}), bf16[8,32,4,3584]{3,2,0,1:T(4,128)(2,1)}, u32[]{:S(2)}, u32[]{:S(2)}) async-start(bf16[8,32,4,3584]{3,2,0,1:T(4,128)(2,1)} %copy.107), calls=%async_computation.2 | async-start | bytes 14680064 | tf_op jit(solution)/shard_map/all_to_all | solution.py:96
  281.1 12.5 %copy_convert_fusion = f32[8,32,4,3584]{3,1,2,0:T(8,128)} fusion(bf16[8,32,4,3584]{3,2,0,1:T(4,128)(2,1)} %all-to-all-done.1), kind=kLoop, calls=%fused_computation.8 | loop fusion | flops 3670016 | bytes 22020096 | tf_op jit(solution)/shard_map/convert_element_type | solution.py:44
  293.6 12.0 %copy.106 = f32[8,32,4,3584]{3,1,0,2:T(8,128)} copy(f32[8,32,4,3584]{3,1,2,0:T(8,128)} %copy_convert_fusion) | data formatting | bytes 29360128 | tf_op jit(solution)/shard_map/convert_element_type | solution.py:44
  305.6 138.2 %all-to-all-done.2 = bf16[8,32,4,3584]{3,2,0,1:T(4,128)(2,1)} async-done(((bf16[8,32,4,3584]{3,2,0,1:T(4,128)(2,1)}), bf16[8,32,4,3584]{3,2,0,1:T(4,128)(2,1)}, u32[]{:S(2)}, u32[]{:S(2)}) %all-to-all-start.2) | async-done | bytes 7340064 | tf_op jit(solution)/shard_map/all_to_all | solution.py:96
  443.8 7.2 copy.108
  451.1 3.2 fusion.19
  454.3 8.3 fusion.22
  462.6 4.1 multiply_convert_fusion.5
  468.8 7.3 convolution_add_fusion
  476.1 19.1 %copy.109 = f32[8,32,4,3584]{3,0,2,1:T(8,128)} copy(f32[8,32,4,3584]{3,1,0,2:T(8,128)} %bitcast.106) | data formatting | bytes 29360128 | tf_op jit(solution)/shard_map/reshape | solution.py:109
  495.2 9.3 all-to-all-start.3
  505.1 7.9 fusion
  513.0 322.6 %all-to-all-done.3 = f32[8,32,4,3584]{3,0,2,1:T(8,128)} async-done(((f32[8,32,4,3584]{3,0,2,1:T(8,128)}), f32[8,32,4,3584]{3,0,2,1:T(8,128)}, u32[]{:S(2)}, u32[]{:S(2)}) %all-to-all-start.3) | async-done | bytes 14680096 | tf_op jit(solution)/shard_map/all_to_all | solution.py:112
  835.6 17.4 %fusion.1 = f32[8,8,3584]{2,1,0:T(8,128)} fusion(f32[8,8,128]{2,1,0:T(8,128)S(1)} %convert_reduce_fusion, f32[8,128,3584]{2,0,1:T(8,128)} %bitcast.20), kind=kOutput, calls=%fused_computation.2 | convolution fusion | flops 352321536 | bytes 15630336 | tf_op jit(solution)/shard_map/gts,gsd->gtd/dot_general | solution.py:118
  853.0 7.3 fusion.3
  861.1 33.3 %all-to-all-start.4 = ((f32[8,32,4]{0,2,1:T(4,128)}), f32[8,32,4]{0,2,1:T(4,128)S(1)}, u32[]{:S(2)}, u32[]{:S(2)}) async-start(f32[8,32,4]{0,2,1:T(4,128)} %copy.111), calls=%async_computation.5 | async-start | bytes 131072 | tf_op jit(solution)/shard_map/all_to_all | solution.py:113
  894.4 7.9 fusion.5
  902.4 7.3 fusion.4
  910.1 14.5 %all-reduce = f32[8,64]{1,0:T(8,128)S(1)} all-reduce(f32[8,64]{1,0:T(8,128)S(1)} %bitcast.108), channel_id=3, replica_groups=mesh['dp'=8,'expert'=32] {'dp'}, use_global_device_ids=true, to_apply=%region_5.6.clone | all-reduce | flops 512 | bytes 4096
  (51 shorter events, 10.1 us)
Async XLA Ops:
  7.2 455.4 %copy-start = (bf16[2,3584,128]{2,1,0:T(8,128)(2,1)S(1)}, bf16[2,3584,128]{2,1,0:T(8,128)(2,1)}, u32[]{:S(2)}) copy-start(bf16[2,3584,128]{2,1,0:T(8,128)(2,1)} %param.12) | copy-start | bytes 5505028
  35.4 52.5 %all-to-all-start = ((bf16[8,32,4]{0,2,1:T(4,128)(2,1)}), bf16[8,32,4]{0,2,1:T(4,128)(2,1)S(1)}, u32[]{:S(2)}, u32[]{:S(2)}) async-start(bf16[8,32,4]{0,2,1:T(4,128)(2,1)} %bitcast.3), calls=%async_computation | async-start | bytes 65536 | tf_op jit(solution)/shard_map/all_to_all | solution.py:98
  87.9 10.0 %copy-start.9 = (bf16[8,3584]{1,0:T(8,128)(2,1)S(1)}, bf16[8,3584]{1,0:T(8,128)(2,1)}, u32[]{:S(2)}) copy-start(bf16[8,3584]{1,0:T(8,128)(2,1)} %param.7) | copy-start | bytes 172036
  87.9 178.6 %all-to-all-start.1 = ((bf16[8,32,4,3584]{3,2,0,1:T(4,128)(2,1)}), bf16[8,32,4,3584]{3,2,0,1:T(4,128)(2,1)}, u32[]{:S(2)}, u32[]{:S(2)}) async-start(bf16[8,32,4,3584]{3,2,0,1:T(4,128)(2,1)} %copy.104), calls=%async_computation.1 | async-start | bytes 14680064 | tf_op jit(solution)/shard_map/all_to_all | solution.py:97
  266.4 177.4 %all-to-all-start.2 = ((bf16[8,32,4,3584]{3,2,0,1:T(4,128)(2,1)}), bf16[8,32,4,3584]{3,2,0,1:T(4,128)(2,1)}, u32[]{:S(2)}, u32[]{:S(2)}) async-start(bf16[8,32,4,3584]{3,2,0,1:T(4,128)(2,1)} %copy.107), calls=%async_computation.2 | async-start | bytes 14680064 | tf_op jit(solution)/shard_map/all_to_all | solution.py:96
  443.8 7.3 copy-start.3
  451.1 11.5 %copy-start.1 = (bf16[8,32,4,3584]{3,1,0,2:T(8,128)(2,1)}, bf16[8,32,4,3584]{3,1,0,2:T(8,128)(2,1)S(1)}, u32[]{:S(2)}) copy-start(bf16[8,32,4,3584]{3,1,0,2:T(8,128)(2,1)S(1)} %copy.108) | copy-start | bytes 22020100
  451.1 3.2 copy-start.2
  466.7 2.1 copy-start.7
  466.7 2.1 copy-start.5
  495.1 9.4 %copy-start.10 = (u32[256]{0:T(256)S(1)}, u32[256]{0:T(256)}, u32[]{:S(2)}) copy-start(u32[256]{0:T(256)} %constant.21) | copy-start | bytes 3076
  495.2 10.0 %copy-start.4 = (bf16[256,2,2,128]{3,0,2,1:T(8,128)(2,1)S(1)}, bf16[256,2,2,128]{3,0,2,1:T(8,128)(2,1)}, u32[]{:S(2)}) copy-start(bf16[256,2,2,128]{3,0,2,1:T(8,128)(2,1)} %get-tuple-element.5) | copy-start | bytes 786436
  495.2 340.4 %all-to-all-start.3 = ((f32[8,32,4,3584]{3,0,2,1:T(8,128)}), f32[8,32,4,3584]{3,0,2,1:T(8,128)}, u32[]{:S(2)}, u32[]{:S(2)}) async-start(f32[8,32,4,3584]{3,0,2,1:T(8,128)} %copy.109), calls=%async_computation.3 | async-start | bytes 29360128 | tf_op jit(solution)/shard_map/all_to_all | solution.py:112
  504.5 421.4 %reduce-scatter.2.cloned.1.call-start = ((), (), s32[]{:S(2)}) async-start(), calls=%async_computation.6 | async-start | bytes 1032192 | tf_op jit(solution)/shard_map/reduce_scatter | solution.py:121
  835.6 17.4 %copy-start.8 = (bf16[256,2,2,128]{3,0,2,1:T(8,128)(2,1)S(1)}, bf16[256,2,2,128]{3,0,2,1:T(8,128)(2,1)}, u32[]{:S(2)}) copy-start(bf16[256,2,2,128]{3,0,2,1:T(8,128)(2,1)} %copy-done.7) | copy-start | bytes 786436
  861.1 48.6 %all-to-all-start.4 = ((f32[8,32,4]{0,2,1:T(4,128)}), f32[8,32,4]{0,2,1:T(4,128)S(1)}, u32[]{:S(2)}, u32[]{:S(2)}) async-start(f32[8,32,4]{0,2,1:T(4,128)} %copy.111), calls=%async_computation.5 | async-start | bytes 131072 | tf_op jit(solution)/shard_map/all_to_all | solution.py:113
  894.4 7.9 copy-start.6
Sparse Core Ops, SparseCore 0:
  853.1 58.7 reduce-scatter.1
where the time goes:
time: 943 us; the launch traced here: 935 us
  waiting for transfers between devices  589 us (62%)
  local copies, waits for them, and re-layouts  87.6 us (9%)
  matrix products  83.5 us (9%)
  starting transfers between devices  78.3 us (8%)
  blocking collectives  66.5 us (7%)
  other arithmetic  15.6 us (2%)
  between operations  14.6 us (2%)
    all_to_all x1, waiting for transfers between devices, local(): lax.all_to_all(token_part, 'expert', split_axis=1, concat_axis=1, tiled=T...  323 us
    all_to_all x1, waiting for transfers between devices, local(): lax.all_to_all(slot_tokens, 'expert', split_axis=1, concat_axis=1, tiled=...  138 us
    all_to_all x1, waiting for transfers between devices, local(): lax.all_to_all(slot_cot, 'expert', split_axis=1, concat_axis=1, tiled=True)  128 us
    all_to_all x1, starting transfers between devices, local(): lax.all_to_all(gate_part, 'expert', split_axis=1, concat_axis=1, tiled=True)  33.3 us
    reshape x2, local copies, waits for them, and re-layouts, local(): slot_cot.reshape(n_groups, n_expert, local_experts * capacity, width)  22.6 us
    reshape x2, local copies, waits for them, and re-layouts, local(): slot_tokens.reshape(n_groups, n_expert, local_experts * capacity, width)  22.5 us
    reshape x1, local copies, waits for them, and re-layouts, local(): token_part.reshape(n_groups, n_expert, local_experts * capacity, width)  19.1 us
  transfers between devices with their start and end apart: 6, of which 3 were waited for; matrix products, arithmetic and copies ran while one was open for 12% of the time, Pallas kernels for 0%

commit v1 on v0

--- a/solution.py
+++ b/solution.py
@@ -74,28 +74,21 @@
     width = tokens.shape[1]
     capacity = 16 * tok_count // experts_all
     slots = experts_all * capacity
-    make_table = partial(route_table, experts_all=experts_all, capacity=capacity)
-    all_tokens, all_cot, all_gates = (
-        lax.all_gather(tokens, "dp", axis=0, tiled=True),
-        lax.all_gather(cotangent, "dp", axis=0, tiled=True),
-        lax.all_gather(gates, "dp", axis=0, tiled=True),
+    per_dest = local_experts * capacity
+    table = route_table(routes, experts_all, capacity)
+    slot_tokens, slot_cot, slot_gates = dispatch(table, tokens, cotangent, gates)
+    slot_tokens = slot_tokens.reshape(n_expert, per_dest, width)
+    slot_cot = slot_cot.reshape(n_expert, per_dest, width)
+    slot_gates = slot_gates.reshape(n_expert, per_dest)
+    recv_tokens, recv_cot, recv_gates = (
+        lax.all_to_all(slot_tokens, "expert", split_axis=0, concat_axis=0, tiled=True),
+        lax.all_to_all(slot_cot, "expert", split_axis=0, concat_axis=0, tiled=True),
+        lax.all_to_all(slot_gates, "expert", split_axis=0, concat_axis=0, tiled=True),
     )
-    all_routes = lax.all_gather(routes, "dp", axis=0, tiled=True)
-    all_routes = all_routes.reshape(n_groups, tok_count, TOPK)
-    tables = jax.vmap(make_table)(all_routes)
-    slot_tokens, slot_cot, slot_gates = jax.vmap(dispatch)(
-        tables,
-        all_tokens.reshape(n_groups, tok_count, width),
-        all_cot.reshape(n_groups, tok_count, width),
-        all_gates.reshape(n_groups, tok_count, TOPK),
-    )
-    slot_tokens = slot_tokens.reshape(n_groups, n_expert, local_experts * capacity, width)
-    slot_cot = slot_cot.reshape(n_groups, n_expert, local_experts * capacity, width)
-    slot_gates = slot_gates.reshape(n_groups, n_expert, local_experts * capacity)
     recv_tokens, recv_cot, recv_gates = (
-        lax.all_to_all(slot_tokens, "expert", split_axis=1, concat_axis=1, tiled=True),
-        lax.all_to_all(slot_cot, "expert", split_axis=1, concat_axis=1, tiled=True),
-        lax.all_to_all(slot_gates, "expert", split_axis=1, concat_axis=1, tiled=True),
+        lax.all_gather(recv_tokens, "dp", axis=0, tiled=True),
+        lax.all_gather(recv_cot, "dp", axis=0, tiled=True),
+        lax.all_gather(recv_gates, "dp", axis=0, tiled=True),
     )
     rows = n_groups * n_expert
     token_part, gate_part, grad_gate, grad_up, grad_down = expert_work(
@@ -106,23 +99,25 @@
         w_up,
         w_down,
     )
-    token_part = token_part.reshape(n_groups, n_expert, local_experts * capacity, width)
-    gate_part = gate_part.reshape(n_groups, n_expert, local_experts * capacity)
+    token_part = token_part.reshape(n_groups, n_expert * per_dest, width)
+    gate_part = gate_part.reshape(n_groups, n_expert * per_dest)
+    token_part, gate_part = (
+        lax.psum_scatter(token_part, "dp", scatter_dimension=0, tiled=False),
+        lax.psum_scatter(gate_part, "dp", scatter_dimension=0, tiled=False),
+    )
+    token_part = token_part.reshape(n_expert, per_dest, width)
+    gate_part = gate_part.reshape(n_expert, per_dest)
     back_tokens, back_gates = (
-        lax.all_to_all(token_part, "expert", split_axis=1, concat_axis=1, tiled=True),
-        lax.all_to_all(gate_part, "expert", split_axis=1, concat_axis=1, tiled=True),
+        lax.all_to_all(token_part, "expert", split_axis=0, concat_axis=0, tiled=True),
+        lax.all_to_all(gate_part, "expert", split_axis=0, concat_axis=0, tiled=True),
     )
-    back_tokens = back_tokens.reshape(n_groups, slots, width)
-    back_gates = back_gates.reshape(n_groups, slots)
-    spread = tables.reshape(n_groups, tok_count, TOPK, slots).sum(axis=2)
-    token_sum = jnp.einsum("gts,gsd->gtd", spread, back_tokens, precision=lax.Precision.HIGHEST)
-    gate_sum = jnp.einsum("gps,gs->gp", tables, back_gates, precision=lax.Precision.HIGHEST)
-    token_total, gate_total = (
-        lax.psum_scatter(token_sum, "dp", scatter_dimension=0, tiled=True),
-        lax.psum_scatter(gate_sum, "dp", scatter_dimension=0, tiled=True),
-    )
-    token_grads = token_total[0].astype(jnp.bfloat16)
-    gate_grads = gate_total[0].reshape(tok_count, TOPK)
+    back_tokens = back_tokens.reshape(slots, width)
+    back_gates = back_gates.reshape(slots)
+    spread = table.reshape(tok_count, TOPK, slots).sum(axis=1)
+    token_sum = jnp.einsum("ts,sd->td", spread, back_tokens, precision=lax.Precision.HIGHEST)
+    gate_sum = jnp.einsum("ps,s->p", table, back_gates, precision=lax.Precision.HIGHEST)
+    token_grads = token_sum.astype(jnp.bfloat16)
+    gate_grads = gate_sum.reshape(tok_count, TOPK)
     return (token_grads, gate_grads, grad_gate, grad_up, grad_down)
 
 

time: 943 us -> 373 us (0.40)
  waiting for transfers between devices: 589 us -> 100 us
  starting transfers between devices: 78.3 us -> 20.3 us
  blocking collectives: 66.5 us -> 108 us
  matrix products: 83.5 us -> 52.5 us
  other arithmetic: 15.6 us -> 1.84 us
  local copies, waits for them, and re-layouts: 87.6 us -> 75.3 us
    all_to_all x5 -> x2, waiting for transfers between devices: 589 us -> 24.1 us  [the longest x1 24.1 us: local(): lax.all_to_all(token_part, 'expert', split_axis=0, concat_axis=0, tiled=T...]
    all_to_all x0 -> x3, blocking collectives: none -> 80.7 us  [the longest x1 36.9 us: local(): lax.all_to_all(slot_tokens, 'expert', split_axis=0, concat_axis=0, tiled=...]
    all_to_all x5 -> x2, starting transfers between devices: 78.3 us -> 20.2 us  [the longest x1 10.1 us: local(): lax.all_to_all(token_part, 'expert', split_axis=0, concat_axis=0, tiled=T...]
    reduce_scatter x1, waiting for transfers between devices: 0.01 us -> 53.3 us  [local(): lax.psum_scatter(token_part, 'dp', scatter_dimension=0, tiled=False)]
    reshape x8 -> x7, local copies, waits for them, and re-layouts: 65 us -> 24.9 us  [the longest x1 17.9 us: local(): token_part = token_part.reshape(n_groups, n_expert * per_dest, width)]
    all_gather x4 -> x1, blocking collectives: 52 us -> 13.4 us  [local(): lax.all_gather(recv_gates, 'dp', axis=0, tiled=True)]
    add x1, local copies, waits for them, and re-layouts: 0.08 us -> 27.1 us  [expert_work(): token_part + jnp.einsum('rjch,jdh->rjcd', grad_upper, w_up, preferred_ele...]
    all_gather x0 -> x2, waiting for transfers between devices: none -> 22.8 us  [the longest x1 22.8 us: local(): lax.all_gather(recv_cot, 'dp', axis=0, tiled=True)]
  transfers between devices with their start and end apart: 6 -> 5, of which waited for: 3 -> 3; matrix products, arithmetic and copies ran while one was open for 12% -> 11% of each run, Pallas kernels for 0% -> 0%
where the time goes in v1:
time: 373 us; the launch traced here: 372 us
  blocking collectives  108 us (29%)
  waiting for transfers between devices  100 us (27%)
  local copies, waits for them, and re-layouts  75.3 us (20%)
  matrix products  52.5 us (14%)
  starting transfers between devices  20.3 us (5%)
  between operations  14 us (4%)
    reduce_scatter x1, waiting for transfers between devices, local(): lax.psum_scatter(token_part, 'dp', scatter_dimension=0, tiled=False)  53.3 us
    all_to_all x1, blocking collectives, local(): lax.all_to_all(slot_tokens, 'expert', split_axis=0, concat_axis=0, tiled=...  36.9 us
    all_to_all x1, blocking collectives, local(): lax.all_to_all(slot_cot, 'expert', split_axis=0, concat_axis=0, tiled=True)  30.3 us
    add x1, local copies, waits for them, and re-layouts, expert_work(): token_part + jnp.einsum('rjch,jdh->rjcd', grad_upper, w_up, preferred_ele...  27.1 us
    all_to_all x1, waiting for transfers between devices, local(): lax.all_to_all(token_part, 'expert', split_axis=0, concat_axis=0, tiled=T...  24.1 us
    all_gather x1, waiting for transfers between devices, local(): lax.all_gather(recv_cot, 'dp', axis=0, tiled=True)  22.8 us
    reshape x1, local copies, waits for them, and re-layouts, local(): token_part = token_part.reshape(n_groups, n_expert * per_dest, width)  17.9 us
    all_to_all x1, blocking collectives, local(): lax.all_to_all(slot_gates, 'expert', split_axis=0, concat_axis=0, tiled=T...  13.5 us
  transfers between devices with their start and end apart: 5, of which 3 were waited for; matrix products, arithmetic and copies ran while one was open for 11% of the time, Pallas kernels for 0%

profile of v1, /device:TPU:32, one launch (start us, length us, event | category | flops | bytes accessed | tf_op | source)
XLA Modules:
  0.0 371.7 jit_solution(14185512726126644538)
XLA Ops:
  9.4 2.2 convolution_convert_fusion
  11.5 1.8 reshape.100
  13.3 36.9 %all_to_all.37 = bf16[32,4,3584]{2,1,0:T(4,128)(2,1)} all-to-all(bf16[32,4,3584]{2,1,0:T(4,128)(2,1)S(1)} %reshape.100), channel_id=1, replica_groups=mesh['dp'=8,'expert'=32] {'expert'}, dimensions={0} | all-to-all | bytes 1835008 | tf_op jit(solution)/shard_map/all_to_all | solution.py:84
  50.4 2.2 convolution_convert_fusion.1
  52.5 1.8 reshape.99
  54.3 30.3 %all_to_all.38 = bf16[32,4,3584]{2,1,0:T(4,128)(2,1)} all-to-all(bf16[32,4,3584]{2,1,0:T(4,128)(2,1)S(1)} %reshape.99), channel_id=1, replica_groups=mesh['dp'=8,'expert'=32] {'expert'}, dimensions={0} | all-to-all | bytes 1835008 | tf_op jit(solution)/shard_map/all_to_all | solution.py:85
  85.1 13.5 %all_to_all.39 = bf16[32,1,4]{2,1,0:T(2,128)(2,1)S(1)} all-to-all(bf16[32,1,4]{2,1,0:T(2,128)(2,1)S(1)} %all_to_all.31), channel_id=1, replica_groups=mesh['dp'=8,'expert'=32] {'expert'}, dimensions={0} | all-to-all | bytes 512 | tf_op jit(solution)/shard_map/all_to_all | solution.py:86
  98.6 13.4 %all-gather = bf16[256,1,4]{2,1,0:T(2,128)(2,1)S(1)} all-gather(bf16[32,1,4]{2,1,0:T(2,128)(2,1)S(1)} %all_to_all.39), channel_id=2, replica_groups=mesh['dp'=8,'expert'=32] {'dp'}, dimensions={0}, use_global_device_ids=true | all-gather | bytes 2304 | tf_op jit(solution)/shard_map/all_gather | solution.py:91
  112.2 4.5 %copy.58 = bf16[256,4,3584]{2,0,1:T(8,128)(2,1)S(1)} copy(bf16[256,4,3584]{2,1,0:T(4,128)(2,1)} %all-gather.6.cloned.1.call-done) | data formatting | bytes 14680064 | tf_op jit(solution)/shard_map/all_gather | solution.py:89
  116.8 3.0 copy-done.2
  119.7 2.1 fusion.26
  121.8 22.8 %all-gather.4.cloned.1.call-done = bf16[256,4,3584]{2,1,0:T(4,128)(2,1)} async-done(((bf16[32,4,3584]{2,1,0:T(4,128)(2,1)}), bf16[256,4,3584]{2,1,0:T(4,128)(2,1)}) %all-gather.4.cloned.1.call-update) | async-done | bytes 7340048 | tf_op jit(solution)/shard_map/all_gather | solution.py:90
  144.6 4.5 %copy.57 = bf16[256,4,3584]{2,0,1:T(8,128)(2,1)S(1)} copy(bf16[256,4,3584]{2,1,0:T(4,128)(2,1)} %all-gather.4.cloned.1.call-done) | data formatting | bytes 14680064 | tf_op jit(solution)/shard_map/all_gather | solution.py:90
  149.2 2.1 fusion.29
  151.3 3.6 copy-done.3
  154.9 2.2 multiply_convert_fusion
  157.1 7.3 %fusion.14 = f32[2,256,2,3584]{3,1,2,0:T(8,128)} fusion(bf16[256,2,2,128]{3,0,2,1:T(8,128)(2,1)S(1)} %get-tuple-element.6, bf16[2,3584,128]{2,1,0:T(8,128)(2,1)S(1)} %copy-done.6), kind=kOutput, calls=%fused_computation.16 | convolution fusion | flops 939524096 | bytes 16777216 | tf_op jit(solution)/shard_map/rjch,jdh->rjcd/dot_general | solution.py:52
  164.4 7.2 %add_bitcast_fusion = f32[256,2,2,3584]{3,0,2,1:T(8,128)S(1)} fusion(f32[2,256,2,3584]{3,1,2,0:T(8,128)} %fusion.14, bf16[256,2,2,128]{3,0,2,1:T(8,128)(2,1)S(1)} %get-tuple-element.7, bf16[2,3584,128]{2,1,0:T(8,128)(2,1)S(1)} %copy-done), kind=kOutput, calls=%fused_computation.4 | convolution fusion | flops 943194112 | bytes 31457280 | tf_op jit(solution)/shard_map/rjch,jdh->rjcd/dot_general | solution.py:53
  171.6 27.1 %copy.59 = f32[256,2,2,3584]{3,2,1,0:T(2,128)} copy(f32[256,2,2,3584]{3,0,2,1:T(8,128)S(1)} %add_bitcast_fusion) | data formatting | bytes 29360128 | tf_op jit(solution)/shard_map/add | solution.py:53
  198.7 17.9 %reshape.102 = f32[8,128,3584]{2,1,0:T(8,128)} reshape(f32[256,2,2,3584]{3,2,1,0:T(2,128)} %copy.59) | data formatting | bytes 29360128 | tf_op jit(solution)/shard_map/reshape | solution.py:102
  218.1 5.2 %fusion.1 = f32[256,2,2]{0,2,1:T(2,128)S(1)} fusion(bf16[256,2,2,3584]{3,0,2,1:T(8,128)(2,1)} %bitcast.95, bf16[256,2,2,128]{3,0,2,1:T(8,128)(2,1)S(1)} %get-tuple-element.5, bf16[2,128,3584]{2,1,0:T(8,128)(2,1)S(1)} %copy-done.9), kind=kOutput, calls=%fused_computation.3 | convolution fusion | flops 950533120 | bytes 9441280 | tf_op jit(solution)/shard_map/rjch,jhd->rjcd/dot_general | solution.py:43
  223.9 13.3 %all-reduce = f32[8,128]{1,0:T(8,128)S(1)} all-reduce(f32[8,128]{1,0:T(8,128)S(1)} %reshape.104), channel_id=4, replica_groups=mesh['dp'=8,'expert'=32] {'dp'}, use_global_device_ids=true, to_apply=%region_5.6.clone | all-reduce | flops 1024 | bytes 8192
  238.6 10.1 %all-to-all-start.4 = ((f32[32,1,4]{2,1,0:T(1,128)}), f32[32,1,4]{2,1,0:T(1,128)S(1)}, u32[]{:S(2)}, u32[]{:S(2)}) async-start(f32[32,1,4]{2,1,0:T(1,128)} %bitcast.18), calls=%async_computation.5 | async-start | bytes 32768 | tf_op jit(solution)/shard_map/all_to_all | solution.py:112
  248.7 53.3 %reduce-scatter.2.cloned.1.call-done = f32[1,128,3584]{2,1,0:T(8,128)} async-done(((f32[8,128,3584]{2,1,0:T(8,128)}), f32[1,128,3584]{2,1,0:T(8,128)}) %reduce-scatter.2.cloned.1.call-update) | async-done | bytes 1835024 | tf_op jit(solution)/shard_map/reduce_scatter | solution.py:105
  302.0 2.9 reshape_reduce_scatter.4
  304.9 10.1 %all-to-all-start.3 = ((f32[32,4,3584]{2,1,0:T(4,128)}), f32[32,4,3584]{2,1,0:T(4,128)}, u32[]{:S(2)}, u32[]{:S(2)}) async-start(f32[32,4,3584]{2,1,0:T(4,128)} %reshape_reduce_scatter.4), calls=%async_computation.4 | async-start | bytes 3670016 | tf_op jit(solution)/shard_map/all_to_all | solution.py:111
  315.0 7.4 %fusion.12 = bf16[2,3584,128]{2,1,0:T(8,128)(2,1)} fusion(bf16[256,2,2,3584]{3,0,2,1:T(8,128)(2,1)} %bitcast.91, bf16[256,2,2,128]{3,0,2,1:T(8,128)(2,1)S(1)} %get-tuple-element.6), kind=kOutput, calls=%fused_computation.11 | convolution fusion | flops 940441600 | bytes 9437184 | tf_op jit(solution)/shard_map/rjcd,rjch->jdh/dot_general | solution.py:56
  322.4 7.4 %fusion.13 = bf16[2,3584,128]{2,1,0:T(8,128)(2,1)} fusion(bf16[256,2,2,3584]{3,0,2,1:T(8,128)(2,1)} %bitcast.92, bf16[256,2,2,128]{3,0,2,1:T(8,128)(2,1)S(1)} %get-tuple-element.7), kind=kOutput, calls=%fused_computation.12 | convolution fusion | flops 940441600 | bytes 9437184 | tf_op jit(solution)/shard_map/rjcd,rjch->jdh/dot_general | solution.py:59
  329.9 2.9 fusion.9
  335.1 24.1 %all-to-all-done.3 = f32[32,4,3584]{2,1,0:T(4,128)} async-done(((f32[32,4,3584]{2,1,0:T(4,128)}), f32[32,4,3584]{2,1,0:T(4,128)}, u32[]{:S(2)}, u32[]{:S(2)}) %all-to-all-start.3) | async-done | bytes 1835040 | tf_op jit(solution)/shard_map/all_to_all | solution.py:111
  359.2 2.9 reshape.103
  362.1 3.1 convolution_convert_fusion.2
  (55 shorter events, 8.5 us)
Async XLA Ops:
  7.2 144.1 %copy-start = (bf16[2,3584,128]{2,1,0:T(8,128)(2,1)S(1)}, bf16[2,3584,128]{2,1,0:T(8,128)(2,1)}, u32[]{:S(2)}) copy-start(bf16[2,3584,128]{2,1,0:T(8,128)(2,1)} %param.12) | copy-start | bytes 5505028
  7.2 77.5 %copy-start.7 = (bf16[8,8]{1,0:T(8,128)(2,1)S(1)}, bf16[8,8]{1,0:T(8,128)(2,1)}, u32[]{:S(2)}) copy-start(bf16[8,8]{1,0:T(8,128)(2,1)} %param.9) | copy-start | bytes 388
  7.2 105.0 %all-gather.6.cloned.1.call-start = ((), (), s32[]{:S(2)}) async-start(), calls=%async_computation.7 | async-start | bytes 8257536 | tf_op jit(solution)/shard_map/all_gather | solution.py:89
  50.3 94.3 %all-gather.4.cloned.1.call-start = ((), (), s32[]{:S(2)}) async-start(), calls=%async_computation.6 | async-start | bytes 8257536 | tf_op jit(solution)/shard_map/all_gather | solution.py:90
  84.6 217.4 %reduce-scatter.2.cloned.1.call-start = ((), (), s32[]{:S(2)}) async-start(), calls=%async_computation.8 | async-start | bytes 16515072 | tf_op jit(solution)/shard_map/reduce_scatter | solution.py:105
  112.2 7.5 %copy-start.5 = (bf16[2,3584,128]{2,1,0:T(8,128)(2,1)S(1)}, bf16[2,3584,128]{2,1,0:T(8,128)(2,1)}, u32[]{:S(2)}) copy-start(bf16[2,3584,128]{2,1,0:T(8,128)(2,1)} %param.11) | copy-start | bytes 5505028
  116.8 3.0 copy-start.2
  144.6 4.6 %copy-start.8 = (bf16[2,128,3584]{2,1,0:T(8,128)(2,1)S(1)}, bf16[2,128,3584]{2,1,0:T(8,128)(2,1)}, u32[]{:S(2)}) copy-start(bf16[2,128,3584]{2,1,0:T(8,128)(2,1)} %param.13) | copy-start | bytes 5505028
  149.1 7.9 %copy-start.4 = (bf16[256,4,3584]{2,0,1:T(8,128)(2,1)}, bf16[256,4,3584]{2,0,1:T(8,128)(2,1)S(1)}, u32[]{:S(2)}) copy-start(bf16[256,4,3584]{2,0,1:T(8,128)(2,1)S(1)} %copy.57) | copy-start | bytes 22020100
  149.2 5.7 %copy-start.3 = (bf16[256,4,3584]{2,0,1:T(8,128)(2,1)S(1)}, bf16[256,4,3584]{2,0,1:T(8,128)(2,1)}, u32[]{:S(2)}) copy-start(bf16[256,4,3584]{2,0,1:T(8,128)(2,1)} %copy-done.2) | copy-start | bytes 22020100
  154.9 2.2 copy-start.6
  216.6 0.7 copy-start.10
  216.6 1.5 copy-start.9
  238.6 66.2 %all-to-all-start.4 = ((f32[32,1,4]{2,1,0:T(1,128)}), f32[32,1,4]{2,1,0:T(1,128)S(1)}, u32[]{:S(2)}, u32[]{:S(2)}) async-start(f32[32,1,4]{2,1,0:T(1,128)} %bitcast.18), calls=%async_computation.5 | async-start | bytes 32768 | tf_op jit(solution)/shard_map/all_to_all | solution.py:112
  304.9 54.3 %all-to-all-start.3 = ((f32[32,4,3584]{2,1,0:T(4,128)}), f32[32,4,3584]{2,1,0:T(4,128)}, u32[]{:S(2)}, u32[]{:S(2)}) async-start(f32[32,4,3584]{2,1,0:T(4,128)} %reshape_reduce_scatter.4), calls=%async_computation.4 | async-start | bytes 3670016 | tf_op jit(solution)/shard_map/all_to_all | solution.py:111
  315.0 14.9 %slice-start = ((s8[7340032]{0:T(1024)(128)(4,1)}), s8[4194304]{0:T(1024)(128)(4,1)S(1)}, s32[]{:S(2)}) async-start(s8[7340032]{0:T(1024)(128)(4,1)} %bitcast.96), calls=%async_computation.9 | async-start | bytes 8388608
  322.4 7.4 %slice-start.1 = ((s8[7340032]{0:T(1024)(128)(4,1)}), s8[3145728]{0:T(1024)(128)(4,1)S(1)}, s32[]{:S(2)}) async-start(s8[7340032]{0:T(1024)(128)(4,1)} %bitcast.96), calls=%async_computation.10 | async-start | bytes 6291456
  322.4 42.7 %copy-start.1 = (bf16[2,3584,128]{2,1,0:T(8,128)(2,1)S(1)}, bf16[2,3584,128]{2,1,0:T(8,128)(2,1)}, u32[]{:S(2)}) copy-start(bf16[2,3584,128]{2,1,0:T(8,128)(2,1)} %param.12) | copy-start | bytes 5505028
Sparse Core Ops, SparseCore 0:
  50.4 44.2 all-gather.5
  96.6 47.9 all-gather.3
  216.8 85.1 reduce-scatter.1

commit v2 on v1

v2 whole, which is shorter than its diff:
```python
from functools import partial

import jax
import jax.numpy as jnp
from jax import lax
from jax.sharding import PartitionSpec as P

TOPK = 8


def route_table(routes, experts_all, capacity):
    pairs = routes.reshape(-1)
    onehot = (pairs[:, None] == jnp.arange(experts_all, dtype=jnp.int32)[None, :]).astype(jnp.int32)
    before = jnp.cumsum(onehot, axis=0) - onehot
    within = jnp.sum(before * onehot, axis=1)
    target = pairs * capacity + within
    slot_ids = jnp.arange(experts_all * capacity, dtype=jnp.int32)
    return (target[:, None] == slot_ids[None, :]).astype(jnp.float32)


def dispatch(table, tokens, cotangent, gates):
    count = tokens.shape[0]
    slots = table.shape[1]
    spread = table.reshape(count, TOPK, slots).sum(axis=1).astype(jnp.bfloat16)
    both = jnp.concatenate([tokens, cotangent], axis=1)
    slot_rows = jnp.einsum(
        "ts,td->sd", spread, both, preferred_element_type=jnp.float32
    ).astype(jnp.bfloat16)
    flat_gates = gates.reshape(-1).astype(jnp.float32)
    slot_gates = jnp.einsum("ps,p->s", table, flat_gates, precision=lax.Precision.HIGHEST).astype(
        jnp.bfloat16
    )
    pad = jnp.zeros((slots, 127), jnp.bfloat16)
    return jnp.concatenate([slot_rows, slot_gates[:, None], pad], axis=1)


def expert_one(rows_in, cot_in, row_gate, w_gate, w_up, w_down):
    gate_pre = jnp.dot(rows_in, w_gate, preferred_element_type=jnp.float32)
    upper_pre = jnp.dot(rows_in, w_up, preferred_element_type=jnp.float32)
    gate_sig = jax.nn.sigmoid(gate_pre)
    active = (gate_pre * gate_sig * upper_pre).astype(jnp.bfloat16)
    output = jnp.dot(active, w_down, preferred_element_type=jnp.float32)
    cot_float = cot_in.astype(jnp.float32)
    gate_part = jnp.sum(output * cot_float, axis=-1)
    scaled = (row_gate.astype(jnp.float32)[:, None] * cot_float).astype(jnp.bfloat16)
    grad_active = lax.dot_general(
        scaled, w_down, (((1,), (1,)), ((), ())), preferred_element_type=jnp.float32
    )
    grad_upper = (grad_active * gate_pre * gate_sig).astype(jnp.bfloat16)
    grad_gpre = (grad_active * upper_pre * gate_sig * (1.0 + gate_pre * (1.0 - gate_sig))).astype(
        jnp.bfloat16
    )
    token_part = lax.dot_general(
        grad_gpre, w_gate, (((1,), (1,)), ((), ())), preferred_element_type=jnp.float32
    )
    token_part = token_part + lax.dot_general(
        grad_upper, w_up, (((1,), (1,)), ((), ())), preferred_element_type=jnp.float32
    )
    grad_g = lax.dot_general(
        rows_in, grad_gpre, (((0,), (0,)), ((), ())), preferred_element_type=jnp.float32
    ).astype(jnp.bfloat16)
    grad_u = lax.dot_general(
        rows_in, grad_upper, (((0,), (0,)), ((), ())), preferred_element_type=jnp.float32
    ).astype(jnp.bfloat16)
    grad_d = lax.dot_general(
        active, scaled, (((0,), (0,)), ((), ())), preferred_element_type=jnp.float32
    ).astype(jnp.bfloat16)
    return (token_part, gate_part, grad_g, grad_u, grad_d)


def local(tokens, routes, gates, cotangent, w_gate, w_up, w_down):
    n_expert = lax.axis_size("expert")
    n_groups = lax.axis_size("dp")
    local_experts = w_gate.shape[0]
    experts_all = local_experts * n_expert
    tok_count = tokens.shape[0]
    width = tokens.shape[1]
    capacity = 16 * tok_count // experts_all
    slots = experts_all * capacity
    per_dest = local_experts * capacity
    table = route_table(routes, experts_all, capacity)
    send = dispatch(table, tokens, cotangent, gates)
    send = send.reshape(n_expert, per_dest, send.shape[-1])
    recv = lax.all_to_all(send, "expert", split_axis=0, concat_axis=0, tiled=True)
    recv = lax.all_gather(recv, "dp", axis=0, tiled=True)
    rows = n_groups * n_expert
    parts, gparts, grads_g, grads_u, grads_d = [], [], [], [], []
    for j in range(local_experts):
        block = recv[:, j * capacity:(j + 1) * capacity, :].reshape(rows * capacity, -1)
        token_part, gate_part, grad_g, grad_u, grad_d = expert_one(
            block[:, :width],
            block[:, width:2 * width],
            block[:, 2 * width],
            w_gate[j],
            w_up[j],
            w_down[j],
        )
        token_part = token_part.reshape(n_groups, n_expert * capacity, width)
        part = lax.psum_scatter(token_part, "dp", scatter_dimension=0, tiled=False)
        parts.append(part.reshape(n_expert, capacity, width))
        gparts.append(gate_part.reshape(n_groups, n_expert, capacity))
        grads_g.append(grad_g)
        grads_u.append(grad_u)
        grads_d.append(grad_d)
    token_part = jnp.stack(parts, axis=1).reshape(n_expert, local_experts, capacity, width)
    gate_part = jnp.stack(gparts, axis=2).reshape(n_groups, n_expert * per_dest)
    gate_part = lax.psum_scatter(gate_part, "dp", scatter_dimension=0, tiled=False)
    gate_part = gate_part.reshape(n_expert, per_dest)
    back_tokens, back_gates = (
        lax.all_to_all(token_part, "expert", split_axis=0, concat_axis=0, tiled=True),
        lax.all_to_all(gate_part, "expert", split_axis=0, concat_axis=0, tiled=True),
    )
    back_tokens = back_tokens.reshape(slots, width)
    back_gates = back_gates.reshape(slots)
    spread = table.reshape(tok_count, TOPK, slots).sum(axis=1)
    token_sum = jnp.einsum("ts,sd->td", spread, back_tokens, precision=lax.Precision.HIGHEST)
    gate_sum = jnp.einsum("ps,s->p", table, back_gates, precision=lax.Precision.HIGHEST)
    token_grads = token_sum.astype(jnp.bfloat16)
    gate_grads = gate_sum.reshape(tok_count, TOPK)
    grad_gate = jnp.stack(grads_g, axis=0)
    grad_up = jnp.stack(grads_u, axis=0)
    grad_down = jnp.stack(grads_d, axis=0)
    return (token_grads, gate_grads, grad_gate, grad_up, grad_down)


def solution(mesh):
    return jax.shard_map(
        local,
        mesh=mesh,
        in_specs=(
            P(("dp", "expert"), None),
            P(("dp", "expert"), None),
            P(("dp", "expert"), None),
            P(("dp", "expert"), None),
            P("expert", None, "dp"),
            P("expert", None, "dp"),
            P("expert", "dp", None),
        ),
        out_specs=(
            P(("dp", "expert"), None),
            P(("dp", "expert"), None),
            P("expert", None, "dp"),
            P("expert", None, "dp"),
            P("expert", "dp", None),
        ),
        check_vma=False,
    )
```

time: 373 us -> 376 us (level)
  waiting for transfers between devices: 100 us -> 129 us
  blocking collectives: 108 us -> 82.5 us
  other arithmetic: 1.84 us -> 11.5 us
  matrix products: 52.5 us -> 45.7 us
  local copies, waits for them, and re-layouts: 75.3 us -> 71 us
    all_gather x2 -> x1, waiting for transfers between devices: 22.8 us -> 76.3 us  [local(): recv = lax.all_gather(recv, 'dp', axis=0, tiled=True)]
    reduce_scatter x1 -> x2, waiting for transfers between devices: 53.3 us -> 24.2 us  [local(): part = lax.psum_scatter(token_part, 'dp', scatter_dimension=0, tiled=False)]
    add x1 -> x0, local copies, waits for them, and re-layouts: 27.1 us -> none  [expert_work(): token_part + jnp.einsum('rjch,jdh->rjcd', grad_upper, w_up, preferred_ele...]
    all_to_all x3 -> x1, blocking collectives: 80.7 us -> 57.3 us  [local(): lax.all_to_all(send, 'expert', split_axis=0, concat_axis=0, tiled=True)]
    slice x0 -> x1, local copies, waits for them, and re-layouts: none -> 16.6 us  [local(): recv[:, j * capacity:(j + 1) * capacity, :].reshape(rows * capacity, -1)]
    all_gather x1 -> x0, blocking collectives: 13.4 us -> none  [local(): lax.all_gather(recv_gates, 'dp', axis=0, tiled=True)]
    unnamed x1, blocking collectives: 13.3 us -> 25.2 us
    reshape x4 -> x2, local copies, waits for them, and re-layouts: 21.8 us -> 31.4 us  [local(): recv[:, j * capacity:(j + 1) * capacity, :].reshape(rows * capacity, -1)]
  transfers between devices with their start and end apart: 5 -> 5, of which waited for: 3 -> 3; matrix products, arithmetic and copies ran while one was open for 11% -> 17% of each run, Pallas kernels for 0% -> 0%
where the time goes in v2:
time: 376 us; the launch traced here: 375 us
  waiting for transfers between devices  129 us (34%)
  blocking collectives  82.5 us (22%)
  local copies, waits for them, and re-layouts  71 us (19%)
  matrix products  45.7 us (12%)
  starting transfers between devices  20.7 us (6%)
  between operations  14.3 us (4%)
  other arithmetic  11.5 us (3%)
    all_gather x1, waiting for transfers between devices, local(): recv = lax.all_gather(recv, 'dp', axis=0, tiled=True)  76.3 us
    all_to_all x1, blocking collectives, local(): lax.all_to_all(send, 'expert', split_axis=0, concat_axis=0, tiled=True)  57.3 us
    reshape x2, local copies, waits for them, and re-layouts, local(): recv[:, j * capacity:(j + 1) * capacity, :].reshape(rows * capacity, -1)  31.4 us
    all_to_all x1, waiting for transfers between devices, local(): lax.all_to_all(token_part, 'expert', split_axis=0, concat_axis=0, tiled=T...  28.2 us
    unnamed x1, blocking collectives  25.2 us
    reduce_scatter x2, waiting for transfers between devices, local(): part = lax.psum_scatter(token_part, 'dp', scatter_dimension=0, tiled=False)  24.2 us
    slice x1, local copies, waits for them, and re-layouts, local(): recv[:, j * capacity:(j + 1) * capacity, :].reshape(rows * capacity, -1)  16.6 us
    all_to_all x1, starting transfers between devices, local(): lax.all_to_all(token_part, 'expert', split_axis=0, concat_axis=0, tiled=T...  10.3 us
  transfers between devices with their start and end apart: 5, of which 3 were waited for; matrix products, arithmetic and copies ran while one was open for 17% of the time, Pallas kernels for 0%

profile of v2, /device:TPU:32, one launch (start us, length us, event | category | flops | bytes accessed | tf_op | source)
XLA Modules:
  0.0 374.6 jit_solution(2525341771582631884)
XLA Ops:
  10.4 1.5 convolution_convert_fusion
  11.9 1.6 concatenate.12
  14.1 5.0 %concatenate.14 = bf16[32,4,7296]{2,1,0:T(4,128)(2,1)S(1)} concatenate(bf16[32,4,7168]{2,1,0:T(4,128)(2,1)} %concatenate.12, bf16[32,4,1]{2,1,0:T(4,128)(2,1)S(1)} %concatenate.15, bf16[32,4,127]{2,1,0:T(4,128)(2,1)S(1)} %broadcast_in_dim.2), dimensions={2} | concatenate | bytes 3735552 | tf_op jit(solution)/shard_map/concatenate | solution.py:34
  19.1 57.3 %all_to_all.19 = bf16[32,4,7296]{2,1,0:T(4,128)(2,1)} all-to-all(bf16[32,4,7296]{2,1,0:T(4,128)(2,1)S(1)} %concatenate.14), channel_id=1, replica_groups=mesh['dp'=8,'expert'=32] {'expert'}, dimensions={0} | all-to-all | bytes 3735552 | tf_op jit(solution)/shard_map/all_to_all | solution.py:84
  76.5 76.3 %all-gather.2.cloned.1.call-done = bf16[256,4,7296]{2,1,0:T(4,128)(2,1)} async-done(((bf16[32,4,7296]{2,1,0:T(4,128)(2,1)}), bf16[256,4,7296]{2,1,0:T(4,128)(2,1)}) %all-gather.2.cloned.1.call-update) | async-done | bytes 14942224 | tf_op jit(solution)/shard_map/all_gather | solution.py:85
  152.8 16.6 %fusion.66 = (bf16[256,2,7296]{2,1,0:T(2,128)(2,1)}, bf16[256,2,7296]{2,1,0:T(2,128)(2,1)}) fusion(bf16[256,4,7296]{2,1,0:T(4,128)(2,1)} %all-gather.2.cloned.1.call-done), kind=kLoop, calls=%fused_computation.100 | loop fusion | bytes 29884416 | tf_op jit(solution)/shard_map/slice | solution.py:89
  169.4 15.7 %reshape.89 = bf16[512,7296]{1,0:T(8,128)(2,1)} reshape(bf16[256,2,7296]{2,1,0:T(2,128)(2,1)} %get-tuple-element.5) | data formatting | bytes 14942208 | tf_op jit(solution)/shard_map/reshape | solution.py:89
  186.3 3.3 fusion.18
  189.7 3.4 fusion.27
  195.5 4.1 %convolution_add_fusion.1 = f32[512,3584]{1,0:T(8,128)} fusion(f32[512,3584]{1,0:T(8,128)S(1)} %fusion.36, bf16[512,128]{1,0:T(8,128)(2,1)S(1)} %get-tuple-element.9, bf16[2,3584,128]{2,1,0:T(8,128)(2,1)S(1)} %copy-done.1), kind=kOutput, calls=%fused_computation.10 | convolution fusion | flops 471597056 | bytes 15728640 | tf_op jit(solution)/shard_map/dot_general | solution.py:56
  199.8 15.7 %reshape.91 = bf16[512,7296]{1,0:T(8,128)(2,1)} reshape(bf16[256,2,7296]{2,1,0:T(2,128)(2,1)} %get-tuple-element.6) | data formatting | bytes 14942208 | tf_op jit(solution)/shard_map/reshape | solution.py:89
  216.7 3.4 fusion.12
  220.1 3.4 fusion.24
  226.1 4.1 %convolution_add_fusion = f32[512,3584]{1,0:T(8,128)} fusion(f32[512,3584]{1,0:T(8,128)S(1)} %fusion.29, bf16[512,128]{1,0:T(8,128)(2,1)S(1)} %get-tuple-element.12, bf16[2,3584,128]{2,1,0:T(8,128)(2,1)S(1)} %copy-done.2), kind=kOutput, calls=%fused_computation.9 | convolution fusion | flops 471597056 | bytes 15728640 | tf_op jit(solution)/shard_map/dot_general | solution.py:56
  231.8 3.3 fusion.1
  235.2 3.3 fusion.3
  239.2 25.2 %all-reduce = f32[8,128]{0,1:T(8,128)S(1)} all-reduce(f32[8,128]{0,1:T(8,128)S(1)} %bitcast.88), channel_id=4, replica_groups=mesh['dp'=8,'expert'=32] {'dp'}, use_global_device_ids=true, to_apply=%region_7.8.clone | all-reduce | flops 1024 | bytes 8192
  266.0 10.1 %all-to-all-start.2 = ((f32[32,1,4]{2,1,0:T(1,128)}), f32[32,1,4]{2,1,0:T(1,128)S(1)}, u32[]{:S(2)}, u32[]{:S(2)}) async-start(f32[32,1,4]{2,1,0:T(1,128)} %bitcast.11), calls=%async_computation.4 | async-start | bytes 32768 | tf_op jit(solution)/shard_map/all_to_all | solution.py:111
  276.1 2.7 stack_reshape_reduce_scatter.6
  278.7 24.2 %reduce-scatter.6.cloned.1.call-done = f32[1,64,3584]{2,1,0:T(8,128)} async-done(((f32[8,64,3584]{2,1,0:T(8,128)}), f32[1,64,3584]{2,1,0:T(8,128)}) %reduce-scatter.6.cloned.1.call-update) | async-done | bytes 917520 | tf_op jit(solution)/shard_map/reduce_scatter | solution.py:99
  302.9 2.6 stack_reshape_reduce_scatter.7
  305.6 3.8 %pad_maximum_fusion = f32[32,2,2,3584]{3,2,1,0:T(2,128)} fusion(f32[32,1,2,3584]{3,2,1,0:T(2,128)} %stack_reshape_reduce_scatter.7, f32[32,1,2,3584]{3,2,1,0:T(2,128)} %stack_reshape_reduce_scatter.6), kind=kLoop, calls=%fused_computation.36 | loop fusion | flops 458752 | bytes 3670016 | tf_op jit(solution)/shard_map/stack | solution.py:105
  309.3 10.3 %all-to-all-start.1 = ((f32[32,2,2,3584]{3,2,1,0:T(2,128)}), f32[32,2,2,3584]{3,2,1,0:T(2,128)}, u32[]{:S(2)}, u32[]{:S(2)}) async-start(f32[32,2,2,3584]{3,2,1,0:T(2,128)} %pad_maximum_fusion), calls=%async_computation.3 | async-start | bytes 3670016 | tf_op jit(solution)/shard_map/all_to_all | solution.py:110
  319.7 3.4 fusion.6
  323.1 1.2 fusion.4
  325.5 1.2 fusion.5
  326.7 1.2 fusion.7
  329.8 1.4 pad_maximum_fusion.3
  331.2 2.2 pad_maximum_fusion.1
  335.7 28.2 %all-to-all-done.1 = f32[32,2,2,3584]{3,2,1,0:T(2,128)} async-done(((f32[32,2,2,3584]{3,2,1,0:T(2,128)}), f32[32,2,2,3584]{3,2,1,0:T(2,128)}, u32[]{:S(2)}, u32[]{:S(2)}) %all-to-all-start.1) | async-done | bytes 1835040 | tf_op jit(solution)/shard_map/all_to_all | solution.py:110
  363.9 2.6 reshape.93
  366.4 1.6 convolution_convert_fusion.7
  (105 shorter events, 20.6 us)
Async XLA Ops:
  7.2 6.4 %copy-start.14 = (bf16[8,8]{1,0:T(8,128)(2,1)S(1)}, bf16[8,8]{1,0:T(8,128)(2,1)}, u32[]{:S(2)}) copy-start(bf16[8,8]{1,0:T(8,128)(2,1)} %param.9) | copy-start | bytes 388
  7.2 145.6 %all-gather.2.cloned.1.call-start = ((), (), s32[]{:S(2)}) async-start(), calls=%async_computation.5 | async-start | bytes 16809984 | tf_op jit(solution)/shard_map/all_gather | solution.py:85
  76.4 199.6 %reduce-scatter.4.cloned.1.call-start = ((), (), s32[]{:S(2)}) async-start(), calls=%async_computation.6 | async-start | bytes 8257536 | tf_op jit(solution)/shard_map/reduce_scatter | solution.py:99
  169.4 16.9 %copy-start = (bf16[2,3584,128]{2,1,0:T(8,128)(2,1)S(1)}, bf16[2,3584,128]{2,1,0:T(8,128)(2,1)}, u32[]{:S(2)}) copy-start(bf16[2,3584,128]{2,1,0:T(8,128)(2,1)} %param.11) | copy-start | bytes 5505028
  185.1 4.5 %copy-start.15 = (bf16[2,128,3584]{2,1,0:T(8,128)(2,1)S(1)}, bf16[2,128,3584]{2,1,0:T(8,128)(2,1)}, u32[]{:S(2)}) copy-start(bf16[2,128,3584]{2,1,0:T(8,128)(2,1)} %param.13) | copy-start | bytes 5505028
  186.3 6.7 %copy-start.10 = (f32[512]{0:T(512)}, f32[512]{0:T(512)S(1)}, u32[]{:S(2)}) copy-start(f32[512]{0:T(512)S(1)} %convert_reduce_fusion.1) | copy-start | bytes 6148
  186.3 6.7 %slice-start = ((s8[7471104]{0:T(1024)(128)(4,1)}), s8[4194304]{0:T(1024)(128)(4,1)S(1)}, s32[]{:S(2)}) async-start(s8[7471104]{0:T(1024)(128)(4,1)} %bitcast.80), calls=%async_computation.8 | async-start | bytes 8388608
  189.6 3.4 slice-start.1
  189.7 3.5 copy-start.1
  194.3 1.1 copy-start.3
  194.3 37.1 %copy-start.19 = (bf16[512,128]{1,0:T(8,128)(2,1)}, bf16[512,128]{1,0:T(8,128)(2,1)S(1)}, u32[]{:S(2)}) copy-start(bf16[512,128]{1,0:T(8,128)(2,1)S(1)} %get-tuple-element.7) | copy-start | bytes 393220
  199.6 103.3 %reduce-scatter.6.cloned.1.call-start = ((), (), s32[]{:S(2)}) async-start(), calls=%async_computation.7 | async-start | bytes 8257536 | tf_op jit(solution)/shard_map/reduce_scatter | solution.py:99
  215.5 4.6 %copy-start.16 = (bf16[2,128,3584]{2,1,0:T(8,128)(2,1)S(1)}, bf16[2,128,3584]{2,1,0:T(8,128)(2,1)}, u32[]{:S(2)}) copy-start(bf16[2,128,3584]{2,1,0:T(8,128)(2,1)} %param.13) | copy-start | bytes 5505028
  216.7 3.4 copy-start.12
  216.7 6.9 %slice-start.4 = ((s8[7471104]{0:T(1024)(128)(4,1)}), s8[4194304]{0:T(1024)(128)(4,1)S(1)}, s32[]{:S(2)}) async-start(s8[7471104]{0:T(1024)(128)(4,1)} %bitcast.84), calls=%async_computation.12 | async-start | bytes 8388608
  220.1 3.5 slice-start.5
  220.1 3.8 %copy-start.2 = (bf16[2,3584,128]{2,1,0:T(8,128)(2,1)S(1)}, bf16[2,3584,128]{2,1,0:T(8,128)(2,1)}, u32[]{:S(2)}) copy-start(bf16[2,3584,128]{2,1,0:T(8,128)(2,1)} %param.12) | copy-start | bytes 5505028
  225.0 1.1 copy-start.4
  225.0 10.2 %copy-start.21 = (bf16[512,128]{1,0:T(8,128)(2,1)}, bf16[512,128]{1,0:T(8,128)(2,1)S(1)}, u32[]{:S(2)}) copy-start(bf16[512,128]{1,0:T(8,128)(2,1)S(1)} %get-tuple-element.10) | copy-start | bytes 393220
  230.2 1.6 copy-start.17
  266.0 43.4 %all-to-all-start.2 = ((f32[32,1,4]{2,1,0:T(1,128)}), f32[32,1,4]{2,1,0:T(1,128)S(1)}, u32[]{:S(2)}, u32[]{:S(2)}) async-start(f32[32,1,4]{2,1,0:T(1,128)} %bitcast.11), calls=%async_computation.4 | async-start | bytes 32768 | tf_op jit(solution)/shard_map/all_to_all | solution.py:111
  305.6 17.5 %slice-start.2 = ((s8[7471104]{0:T(1024)(128)(4,1)}), s8[3276800]{0:T(1024)(128)(4,1)S(1)}, s32[]{:S(2)}) async-start(s8[7471104]{0:T(1024)(128)(4,1)} %bitcast.82), calls=%async_computation.10 | async-start | bytes 6553600
  309.3 54.5 %all-to-all-start.1 = ((f32[32,2,2,3584]{3,2,1,0:T(2,128)}), f32[32,2,2,3584]{3,2,1,0:T(2,128)}, u32[]{:S(2)}, u32[]{:S(2)}) async-start(f32[32,2,2,3584]{3,2,1,0:T(2,128)} %pad_maximum_fusion), calls=%async_computation.3 | async-start | bytes 3670016 | tf_op jit(solution)/shard_map/all_to_all | solution.py:110
  319.7 3.4 slice-start.3
  319.7 4.6 %slice-start.6 = ((s8[7471104]{0:T(1024)(128)(4,1)}), s8[4194304]{0:T(1024)(128)(4,1)S(1)}, s32[]{:S(2)}) async-start(s8[7471104]{0:T(1024)(128)(4,1)} %bitcast.86), calls=%async_computation.14 | async-start | bytes 8388608
  323.1 2.4 slice-start.7
  325.5 1.2 copy-start.5
  326.6 1.2 copy-start.11
  326.7 1.2 copy-start.20
  327.9 0.9 copy-start.13
  331.2 3.5 copy-start.9
  333.3 33.1 %copy-start.7 = (f32[8,128]{1,0:T(8,128)S(1)}, f32[8,128]{1,0:T(8,128)}, u32[]{:S(2)}) copy-start(f32[8,128]{1,0:T(8,128)} %copy-done.6) | copy-start | bytes 12292
  (4 other events, 2.8 us)
Sparse Core Ops, SparseCore 0:
  76.6 76.1 all-gather.1
  199.7 50.7 reduce-scatter.3
  253.0 49.8 reduce-scatter.5

commit v3 on v1

v3 whole, which is shorter than its diff:
```python
from functools import partial

import jax
import jax.numpy as jnp
from jax import lax
from jax.sharding import PartitionSpec as P

TOPK = 8


def route_table(routes, experts_all, capacity):
    pairs = routes.reshape(-1)
    onehot = (pairs[:, None] == jnp.arange(experts_all, dtype=jnp.int32)[None, :]).astype(jnp.int32)
    before = jnp.cumsum(onehot, axis=0) - onehot
    within = jnp.sum(before * onehot, axis=1)
    target = pairs * capacity + within
    slot_ids = jnp.arange(experts_all * capacity, dtype=jnp.int32)
    return (target[:, None] == slot_ids[None, :]).astype(jnp.float32)


def dispatch(table, tokens, cotangent, gates):
    count = tokens.shape[0]
    slots = table.shape[1]
    spread = table.reshape(count, TOPK, slots).sum(axis=1).astype(jnp.bfloat16)
    both = jnp.concatenate([tokens, cotangent], axis=1)
    slot_rows = jnp.einsum(
        "ts,td->sd", spread, both, preferred_element_type=jnp.float32
    ).astype(jnp.bfloat16)
    flat_gates = gates.reshape(-1).astype(jnp.float32)
    slot_gates = jnp.einsum("ps,p->s", table, flat_gates, precision=lax.Precision.HIGHEST).astype(
        jnp.bfloat16
    )
    pad = jnp.zeros((slots, 127), jnp.bfloat16)
    return jnp.concatenate([slot_rows, slot_gates[:, None], pad], axis=1)


def expert_work(recv, w_gate, w_up, w_down, width, capacity):
    rows = recv.shape[0]
    local_experts = w_gate.shape[0]
    blocks = recv.reshape(rows, local_experts, capacity, recv.shape[-1])
    slot_tokens = blocks[..., :width]
    slot_cot = blocks[..., width:2 * width]
    slot_gates = blocks[..., 2 * width]
    gate_pre = jnp.einsum("rjcd,jdh->rjch", slot_tokens, w_gate, preferred_element_type=jnp.float32)
    upper_pre = jnp.einsum("rjcd,jdh->rjch", slot_tokens, w_up, preferred_element_type=jnp.float32)
    gate_sig = jax.nn.sigmoid(gate_pre)
    active = (gate_pre * gate_sig * upper_pre).astype(jnp.bfloat16)
    output = jnp.einsum("rjch,jhd->rjcd", active, w_down, preferred_element_type=jnp.float32)
    cot_float = slot_cot.astype(jnp.float32)
    gate_part = jnp.sum(output * cot_float, axis=-1)
    scaled = (slot_gates.astype(jnp.float32)[..., None] * cot_float).astype(jnp.bfloat16)
    grad_active = jnp.einsum("rjcd,jhd->rjch", scaled, w_down, preferred_element_type=jnp.float32)
    grad_upper = (grad_active * gate_pre * gate_sig).astype(jnp.bfloat16)
    grad_gpre = (grad_active * upper_pre * gate_sig * (1.0 + gate_pre * (1.0 - gate_sig))).astype(
        jnp.bfloat16
    )
    grad_g = jnp.einsum(
        "rjcd,rjch->jdh", slot_tokens, grad_gpre, preferred_element_type=jnp.float32
    ).astype(jnp.bfloat16)
    grad_u = jnp.einsum(
        "rjcd,rjch->jdh", slot_tokens, grad_upper, preferred_element_type=jnp.float32
    ).astype(jnp.bfloat16)
    grad_d = jnp.einsum(
        "rjch,rjcd->jhd", active, scaled, preferred_element_type=jnp.float32
    ).astype(jnp.bfloat16)
    parts = []
    for j in range(local_experts):
        gpre_j = grad_gpre[:, j].reshape(rows * capacity, -1)
        upper_j = grad_upper[:, j].reshape(rows * capacity, -1)
        token_part = lax.dot_general(
            gpre_j, w_gate[j], (((1,), (1,)), ((), ())), preferred_element_type=jnp.float32
        )
        token_part = token_part + lax.dot_general(
            upper_j, w_up[j], (((1,), (1,)), ((), ())), preferred_element_type=jnp.float32
        )
        gate_col = gate_part[:, j].reshape(rows * capacity, 1)
        pad = jnp.zeros((rows * capacity, 127), jnp.float32)
        parts.append(jnp.concatenate([token_part, gate_col, pad], axis=1))
    return (parts, grad_g, grad_u, grad_d)


def local(tokens, routes, gates, cotangent, w_gate, w_up, w_down):
    n_expert = lax.axis_size("expert")
    n_groups = lax.axis_size("dp")
    local_experts = w_gate.shape[0]
    experts_all = local_experts * n_expert
    tok_count = tokens.shape[0]
    width = tokens.shape[1]
    capacity = 16 * tok_count // experts_all
    slots = experts_all * capacity
    per_dest = local_experts * capacity
    table = route_table(routes, experts_all, capacity)
    send = dispatch(table, tokens, cotangent, gates)
    send = send.reshape(n_expert, per_dest, send.shape[-1])
    recv = lax.all_to_all(send, "expert", split_axis=0, concat_axis=0, tiled=True)
    recv = lax.all_gather(recv, "dp", axis=0, tiled=True)
    parts, grad_gate, grad_up, grad_down = expert_work(recv, w_gate, w_up, w_down, width, capacity)
    wide = parts[0].shape[-1]
    summed = []
    for part in parts:
        part = part.reshape(n_groups, n_expert * capacity, wide)
        part = lax.psum_scatter(part, "dp", scatter_dimension=0, tiled=False)
        summed.append(part.reshape(n_expert, capacity, wide))
    back = jnp.stack(summed, axis=1)
    back = lax.all_to_all(back, "expert", split_axis=0, concat_axis=0, tiled=True)
    back = back.reshape(slots, wide)
    back_tokens = back[:, :width]
    back_gates = back[:, width]
    spread = table.reshape(tok_count, TOPK, slots).sum(axis=1)
    token_sum = jnp.einsum("ts,sd->td", spread, back_tokens, precision=lax.Precision.HIGHEST)
    gate_sum = jnp.einsum("ps,s->p", table, back_gates, precision=lax.Precision.HIGHEST)
    token_grads = token_sum.astype(jnp.bfloat16)
    gate_grads = gate_sum.reshape(tok_count, TOPK)
    return (token_grads, gate_grads, grad_gate, grad_up, grad_down)


def solution(mesh):
    return jax.shard_map(
        local,
        mesh=mesh,
        in_specs=(
            P(("dp", "expert"), None),
            P(("dp", "expert"), None),
            P(("dp", "expert"), None),
            P(("dp", "expert"), None),
            P("expert", None, "dp"),
            P("expert", None, "dp"),
            P("expert", "dp", None),
        ),
        out_specs=(
            P(("dp", "expert"), None),
            P(("dp", "expert"), None),
            P("expert", None, "dp"),
            P("expert", None, "dp"),
            P("expert", "dp", None),
        ),
        check_vma=False,
    )
```

time: 373 us -> 372 us (level)
  waiting for transfers between devices: 100 us -> 188 us
  blocking collectives: 108 us -> 57.5 us
  local copies, waits for them, and re-layouts: 75.3 us -> 46.8 us
  starting transfers between devices: 20.3 us -> 10.4 us
    all_gather x2 -> x1, waiting for transfers between devices: 22.8 us -> 76.3 us  [local(): recv = lax.all_gather(recv, 'dp', axis=0, tiled=True)]
    reduce_scatter x1 -> x2, waiting for transfers between devices: 53.3 us -> 86.8 us  [local(): part = lax.psum_scatter(part, 'dp', scatter_dimension=0, tiled=False)]
    concatenate x0 -> x8, local copies, waits for them, and re-layouts: none -> 27.7 us  [the longest x5 17.2 us: expert_work(): parts.append(jnp.concatenate([token_part, gate_col, pad], axis=1))]
    add x1 -> x0, local copies, waits for them, and re-layouts: 27.1 us -> none  [expert_work(): token_part + jnp.einsum('rjch,jdh->rjcd', grad_upper, w_up, preferred_ele...]
    all_to_all x3 -> x1, blocking collectives: 80.7 us -> 57.5 us  [local(): lax.all_to_all(send, 'expert', split_axis=0, concat_axis=0, tiled=True)]
    reshape x6 -> x1, local copies, waits for them, and re-layouts: 24.8 us -> 3.5 us  [local(): back = back.reshape(slots, wide)]
    all_gather x1 -> x0, blocking collectives: 13.4 us -> none  [local(): lax.all_gather(recv_gates, 'dp', axis=0, tiled=True)]
    unnamed x1 -> x0, blocking collectives: 13.3 us -> none
  transfers between devices with their start and end apart: 5 -> 4, of which waited for: 3 -> 4; matrix products, arithmetic and copies ran while one was open for 11% -> 11% of each run, Pallas kernels for 0% -> 0%
where the time goes in v3:
time: 372 us; the launch traced here: 371 us
  waiting for transfers between devices  188 us (51%)
  blocking collectives  57.5 us (15%)
  matrix products  50.3 us (14%)
  local copies, waits for them, and re-layouts  46.8 us (13%)
  between operations  14 us (4%)
  starting transfers between devices  10.4 us (3%)
    reduce_scatter x2, waiting for transfers between devices, local(): part = lax.psum_scatter(part, 'dp', scatter_dimension=0, tiled=False)  86.8 us
    all_gather x1, waiting for transfers between devices, local(): recv = lax.all_gather(recv, 'dp', axis=0, tiled=True)  76.3 us
    all_to_all x1, blocking collectives, local(): lax.all_to_all(send, 'expert', split_axis=0, concat_axis=0, tiled=True)  57.5 us
    all_to_all x1, waiting for transfers between devices, local(): lax.all_to_all(back, 'expert', split_axis=0, concat_axis=0, tiled=True)  24.9 us
    concatenate x5, local copies, waits for them, and re-layouts, expert_work(): parts.append(jnp.concatenate([token_part, gate_col, pad], axis=1))  17.2 us
    concatenate x3, local copies, waits for them, and re-layouts, dispatch(): return jnp.concatenate([slot_rows, slot_gates[:, None], pad], axis=1)  10.5 us
    all_to_all x1, starting transfers between devices, local(): lax.all_to_all(back, 'expert', split_axis=0, concat_axis=0, tiled=True)  10.1 us
    dot_general x2, matrix products, expert_work(): lax.dot_general(upper_j, w_up[j], (((1,), (1,)), ((), ())), preferred_ele...  9.34 us
  transfers between devices with their start and end apart: 4, of which 4 were waited for; matrix products, arithmetic and copies ran while one was open for 11% of the time, Pallas kernels for 0%

profile of v3, /device:TPU:32, one launch (start us, length us, event | category | flops | bytes accessed | tf_op | source)
XLA Modules:
  0.0 370.6 jit_solution(10648942447667212689)
XLA Ops:
  7.2 0.9 eq.57
  10.6 2.8 convolution_convert_fusion
  13.3 4.0 %concatenate.30 = bf16[32,4,7168]{2,1,0:T(4,128)(2,1)} reshape(bf16[128,7168]{1,0:T(8,128)(2,1)} %convolution_convert_fusion) | data formatting | bytes 3670016 | tf_op jit(solution)/shard_map/concatenate | solution.py:34
  17.4 6.2 %concatenate.32 = bf16[32,4,7296]{2,1,0:T(4,128)(2,1)} concatenate(bf16[32,4,7168]{2,1,0:T(4,128)(2,1)} %concatenate.30, bf16[32,4,1]{2,1,0:T(4,128)(2,1)S(1)} %concatenate.40, bf16[32,4,127]{2,1,0:T(4,128)(2,1)S(1)} %broadcast_in_dim.2), dimensions={2} | concatenate | bytes 3735552 | tf_op jit(solution)/shard_map/concatenate | solution.py:34
  23.6 57.5 %all_to_all.10 = bf16[32,4,7296]{2,1,0:T(4,128)(2,1)} all-to-all(bf16[32,4,7296]{2,1,0:T(4,128)(2,1)} %concatenate.32), channel_id=1, replica_groups=mesh['dp'=8,'expert'=32] {'expert'}, dimensions={0} | all-to-all | bytes 3735552 | tf_op jit(solution)/shard_map/all_to_all | solution.py:95
  81.2 76.3 %all-gather.2.cloned.1.call-done = bf16[256,4,7296]{2,1,0:T(4,128)(2,1)} async-done(((bf16[32,4,7296]{2,1,0:T(4,128)(2,1)}), bf16[256,4,7296]{2,1,0:T(4,128)(2,1)}) %all-gather.2.cloned.1.call-update) | async-done | bytes 14942224 | tf_op jit(solution)/shard_map/all_gather | solution.py:96
  157.5 7.0 %copy.55 = bf16[256,4,7296]{2,0,1:T(8,128)(2,1)S(1)} copy(bf16[256,4,7296]{2,1,0:T(4,128)(2,1)} %all-gather.2.cloned.1.call-done) | data formatting | bytes 29884416 | tf_op jit(solution)/shard_map/all_gather | solution.py:96
  164.7 2.1 fusion.30
  166.8 2.1 fusion.35
  168.9 0.8 copy-done.4
  169.7 2.2 multiply_convert_fusion
  172.6 2.4 fusion.1
  175.6 2.3 fusion.45
  177.9 4.1 %convolution_add_fusion.1 = f32[512,3584]{1,0:T(8,128)} fusion(f32[512,3584]{1,0:T(8,128)S(1)} %fusion.45, bf16[512,128]{1,0:T(8,128)(2,1)S(1)} %bitcast.106, bf16[2,3584,128]{2,1,0:T(8,128)(2,1)S(1)} %copy-done.5), kind=kOutput, calls=%fused_computation.6 | convolution fusion | flops 471597056 | bytes 15728640 | tf_op jit(solution)/shard_map/dot_general | solution.py:73
  182.0 8.5 %concatenate.36 = f32[8,64,3712]{2,1,0:T(8,128)} concatenate(f32[8,64,3584]{2,1,0:T(8,128)} %bitcast.93, f32[8,64,1]{2,1,0:T(8,128)S(1)} %concatenate.41, f32[8,64,127]{2,1,0:T(8,128)S(1)} %concatenate.35), dimensions={2} | concatenate | bytes 15204352 | tf_op jit(solution)/shard_map/concatenate | solution.py:78
  191.3 2.3 fusion.42
  193.6 5.3 %convolution_add_fusion = f32[512,3584]{1,0:T(8,128)} fusion(f32[512,3584]{1,0:T(8,128)S(1)} %fusion.42, bf16[512,128]{1,0:T(8,128)(2,1)S(1)} %bitcast.105, bf16[2,3584,128]{2,1,0:T(8,128)(2,1)} %param.12), kind=kOutput, calls=%fused_computation.5 | convolution fusion | flops 471597056 | bytes 15728640 | tf_op jit(solution)/shard_map/dot_general | solution.py:73
  198.8 8.5 %concatenate.39 = f32[8,64,3712]{2,1,0:T(8,128)} concatenate(f32[8,64,3584]{2,1,0:T(8,128)} %bitcast.94, f32[8,64,1]{2,1,0:T(8,128)S(1)} %concatenate.42, f32[8,64,127]{2,1,0:T(8,128)S(1)} %concatenate.35), dimensions={2} | concatenate | bytes 15204352 | tf_op jit(solution)/shard_map/concatenate | solution.py:78
  207.4 35.0 %reduce-scatter.3.cloned.1.call-done = f32[1,64,3712]{2,1,0:T(8,128)} async-done(((f32[8,64,3712]{2,1,0:T(8,128)}), f32[1,64,3712]{2,1,0:T(8,128)}) %reduce-scatter.3.cloned.1.call-update) | async-done | bytes 950288 | tf_op jit(solution)/shard_map/reduce_scatter | solution.py:102
  242.4 1.7 stack_reshape_reduce_scatter.6
  244.2 51.8 %reduce-scatter.5.cloned.1.call-done = f32[1,64,3712]{2,1,0:T(8,128)} async-done(((f32[8,64,3712]{2,1,0:T(8,128)}), f32[1,64,3712]{2,1,0:T(8,128)}) %reduce-scatter.5.cloned.1.call-update) | async-done | bytes 950288 | tf_op jit(solution)/shard_map/reduce_scatter | solution.py:102
  296.0 1.7 stack_reshape_reduce_scatter.7
  297.7 2.2 pad_maximum_fusion
  299.9 10.1 %all-to-all-start.1 = ((f32[32,2,2,3712]{3,2,1,0:T(2,128)}), f32[32,2,2,3712]{3,2,1,0:T(2,128)}, u32[]{:S(2)}, u32[]{:S(2)}) async-start(f32[32,2,2,3712]{3,2,1,0:T(2,128)} %pad_maximum_fusion), calls=%async_computation.3 | async-start | bytes 3801088 | tf_op jit(solution)/shard_map/all_to_all | solution.py:105
  310.1 7.3 %fusion.9 = bf16[2,3584,128]{2,1,0:T(8,128)(2,1)} fusion(bf16[256,2,2,128]{3,0,2,1:T(8,128)(2,1)S(1)} %get-tuple-element.6, bf16[256,2,2,7296]{3,0,2,1:T(8,128)(2,1)} %bitcast.100), kind=kOutput, calls=%fused_computation.12 | convolution fusion | flops 940441600 | bytes 9437184 | tf_op jit(solution)/shard_map/rjcd,rjch->jdh/dot_general | solution.py:57
  317.3 7.4 %fusion.10 = bf16[2,3584,128]{2,1,0:T(8,128)(2,1)} fusion(bf16[256,2,2,128]{3,0,2,1:T(8,128)(2,1)S(1)} %get-tuple-element.7, bf16[256,2,2,7296]{3,0,2,1:T(8,128)(2,1)} %bitcast.101), kind=kOutput, calls=%fused_computation.13 | convolution fusion | flops 940441600 | bytes 9437184 | tf_op jit(solution)/shard_map/rjcd,rjch->jdh/dot_general | solution.py:60
  324.8 5.9 %fusion.11 = bf16[2,128,3584]{2,1,0:T(8,128)(2,1)} fusion(bf16[256,2,2,128]{3,0,2,1:T(8,128)(2,1)S(1)} %copy-done.7, f32[256,2,2]{0,2,1:T(2,128)S(1)} %convert_reduce_fusion, bf16[256,2,2,7296]{3,0,2,1:T(8,128)(2,1)} %bitcast.102), kind=kOutput, calls=%fused_computation.14 | convolution fusion | flops 951451648 | bytes 9441280 | tf_op jit(solution)/shard_map/rjch,rjcd->jhd/dot_general | solution.py:63
  330.6 24.9 %all-to-all-done.1 = f32[32,2,2,3712]{3,2,1,0:T(2,128)} async-done(((f32[32,2,2,3712]{3,2,1,0:T(2,128)}), f32[32,2,2,3712]{3,2,1,0:T(2,128)}, u32[]{:S(2)}, u32[]{:S(2)}) %all-to-all-start.1) | async-done | bytes 1900576 | tf_op jit(solution)/shard_map/all_to_all | solution.py:105
  355.5 3.5 reshape.81
  359.0 0.9 slice_reduce_fusion
  360.0 3.1 convolution_convert_fusion.1
  363.1 1.0 fusion.56
  (44 shorter events, 4.7 us)
Async XLA Ops:
  7.2 159.6 %copy-start = (bf16[2,128,3584]{2,1,0:T(8,128)(2,1)S(1)}, bf16[2,128,3584]{2,1,0:T(8,128)(2,1)}, u32[]{:S(2)}) copy-start(bf16[2,128,3584]{2,1,0:T(8,128)(2,1)} %param.13) | copy-start | bytes 5505028
  7.2 150.3 %all-gather.2.cloned.1.call-start = ((), (), s32[]{:S(2)}) async-start(), calls=%async_computation.4 | async-start | bytes 16809984 | tf_op jit(solution)/shard_map/all_gather | solution.py:96
  81.1 161.3 %reduce-scatter.3.cloned.1.call-start = ((), (), s32[]{:S(2)}) async-start(), calls=%async_computation.5 | async-start | bytes 8552448 | tf_op jit(solution)/shard_map/reduce_scatter | solution.py:102
  157.5 7.2 %copy-start.3 = (bf16[2,3584,128]{2,1,0:T(8,128)(2,1)S(1)}, bf16[2,3584,128]{2,1,0:T(8,128)(2,1)}, u32[]{:S(2)}) copy-start(bf16[2,3584,128]{2,1,0:T(8,128)(2,1)} %param.11) | copy-start | bytes 5505028
  164.5 7.3 %copy-start.2 = (bf16[256,4,7296]{2,0,1:T(8,128)(2,1)}, bf16[256,4,7296]{2,0,1:T(8,128)(2,1)S(1)}, u32[]{:S(2)}) copy-start(bf16[256,4,7296]{2,0,1:T(8,128)(2,1)S(1)} %copy.55) | copy-start | bytes 44826628
  166.8 2.9 copy-start.4
  171.9 0.7 copy-start.6
  175.0 2.9 copy-start.5
  190.5 105.5 %reduce-scatter.5.cloned.1.call-start = ((), (), s32[]{:S(2)}) async-start(), calls=%async_computation.6 | async-start | bytes 8552448 | tf_op jit(solution)/shard_map/reduce_scatter | solution.py:102
  299.9 55.6 %all-to-all-start.1 = ((f32[32,2,2,3712]{3,2,1,0:T(2,128)}), f32[32,2,2,3712]{3,2,1,0:T(2,128)}, u32[]{:S(2)}, u32[]{:S(2)}) async-start(f32[32,2,2,3712]{3,2,1,0:T(2,128)} %pad_maximum_fusion), calls=%async_computation.3 | async-start | bytes 3801088 | tf_op jit(solution)/shard_map/all_to_all | solution.py:105
  317.3 7.4 %copy-start.7 = (bf16[256,2,2,128]{3,0,2,1:T(8,128)(2,1)S(1)}, bf16[256,2,2,128]{3,0,2,1:T(8,128)(2,1)}, u32[]{:S(2)}) copy-start(bf16[256,2,2,128]{3,0,2,1:T(8,128)(2,1)} %copy-done.6) | copy-start | bytes 786436
  317.3 46.8 %copy-start.1 = (bf16[2,128,3584]{2,1,0:T(8,128)(2,1)S(1)}, bf16[2,128,3584]{2,1,0:T(8,128)(2,1)}, u32[]{:S(2)}) copy-start(bf16[2,128,3584]{2,1,0:T(8,128)(2,1)} %param.13) | copy-start | bytes 5505028
Sparse Core Ops, SparseCore 0:
  81.3 76.2 all-gather.1
  190.6 51.8 reduce-scatter.2
  245.0 50.9 reduce-scatter.4

commit v4 on v2

--- a/solution.py
+++ b/solution.py
@@ -77,16 +77,15 @@
     width = tokens.shape[1]
     capacity = 16 * tok_count // experts_all
     slots = experts_all * capacity
-    per_dest = local_experts * capacity
     table = route_table(routes, experts_all, capacity)
     send = dispatch(table, tokens, cotangent, gates)
-    send = send.reshape(n_expert, per_dest, send.shape[-1])
-    recv = lax.all_to_all(send, "expert", split_axis=0, concat_axis=0, tiled=True)
-    recv = lax.all_gather(recv, "dp", axis=0, tiled=True)
+    send = send.reshape(n_expert, local_experts, capacity, send.shape[-1])
     rows = n_groups * n_expert
-    parts, gparts, grads_g, grads_u, grads_d = [], [], [], [], []
+    summed, grads_g, grads_u, grads_d = [], [], [], []
     for j in range(local_experts):
-        block = recv[:, j * capacity:(j + 1) * capacity, :].reshape(rows * capacity, -1)
+        piece = send[:, j].reshape(n_expert * capacity, send.shape[-1])
+        recv = lax.all_to_all(piece, "expert", split_axis=0, concat_axis=0, tiled=True)
+        block = lax.all_gather(recv, "dp", axis=0, tiled=True)
         token_part, gate_part, grad_g, grad_u, grad_d = expert_one(
             block[:, :width],
             block[:, width:2 * width],
@@ -95,23 +94,20 @@
             w_up[j],
             w_down[j],
         )
-        token_part = token_part.reshape(n_groups, n_expert * capacity, width)
-        part = lax.psum_scatter(token_part, "dp", scatter_dimension=0, tiled=False)
-        parts.append(part.reshape(n_expert, capacity, width))
-        gparts.append(gate_part.reshape(n_groups, n_expert, capacity))
+        pad = jnp.zeros((rows * capacity, 127), jnp.float32)
+        part = jnp.concatenate([token_part, gate_part[:, None], pad], axis=1)
+        wide = part.shape[-1]
+        part = part.reshape(n_groups, n_expert * capacity, wide)
+        part = lax.psum_scatter(part, "dp", scatter_dimension=0, tiled=False)
+        summed.append(part.reshape(n_expert, capacity, wide))
         grads_g.append(grad_g)
         grads_u.append(grad_u)
         grads_d.append(grad_d)
-    token_part = jnp.stack(parts, axis=1).reshape(n_expert, local_experts, capacity, width)
-    gate_part = jnp.stack(gparts, axis=2).reshape(n_groups, n_expert * per_dest)
-    gate_part = lax.psum_scatter(gate_part, "dp", scatter_dimension=0, tiled=False)
-    gate_part = gate_part.reshape(n_expert, per_dest)
-    back_tokens, back_gates = (
-        lax.all_to_all(token_part, "expert", split_axis=0, concat_axis=0, tiled=True),
-        lax.all_to_all(gate_part, "expert", split_axis=0, concat_axis=0, tiled=True),
-    )
-    back_tokens = back_tokens.reshape(slots, width)
-    back_gates = back_gates.reshape(slots)
+    back = jnp.stack(summed, axis=1)
+    back = lax.all_to_all(back, "expert", split_axis=0, concat_axis=0, tiled=True)
+    back = back.reshape(slots, back.shape[-1])
+    back_tokens = back[:, :width]
+    back_gates = back[:, width]
     spread = table.reshape(tok_count, TOPK, slots).sum(axis=1)
     token_sum = jnp.einsum("ts,sd->td", spread, back_tokens, precision=lax.Precision.HIGHEST)
     gate_sum = jnp.einsum("ps,s->p", table, back_gates, precision=lax.Precision.HIGHEST)

time: 376 us -> 341 us (0.907)
  local copies, waits for them, and re-layouts: 71 us -> 42.8 us
  waiting for transfers between devices: 129 us -> 147 us
  blocking collectives: 82.5 us -> 67.7 us
  starting transfers between devices: 20.7 us -> 10.4 us
    reduce_scatter x2, waiting for transfers between devices: 24.2 us -> 80.9 us  [local(): part = lax.psum_scatter(part, 'dp', scatter_dimension=0, tiled=False)]
    all_gather x1 -> x2, waiting for transfers between devices: 76.3 us -> 38 us  [local(): block = lax.all_gather(recv, 'dp', axis=0, tiled=True)]
    reshape x4 -> x1, local copies, waits for them, and re-layouts: 34.1 us -> 2.58 us  [local(): back = back.reshape(slots, back.shape[-1])]
    unnamed x1 -> x0, blocking collectives: 25.2 us -> none
    concatenate x0 -> x5, local copies, waits for them, and re-layouts: none -> 17.4 us  [local(): part = jnp.concatenate([token_part, gate_part[:, None], pad], axis=1)]
    slice x1, local copies, waits for them, and re-layouts: 16.6 us -> 0.94 us  [local(): back_gates = back[:, width]]
    all_to_all x1 -> x2, blocking collectives: 57.3 us -> 67.7 us  [local(): lax.all_to_all(piece, 'expert', split_axis=0, concat_axis=0, tiled=True)]
    all_to_all x2 -> x1, starting transfers between devices: 20.4 us -> 10.1 us  [local(): lax.all_to_all(back, 'expert', split_axis=0, concat_axis=0, tiled=True)]
  transfers between devices with their start and end apart: 5 -> 5, of which waited for: 3 -> 5; matrix products, arithmetic and copies ran while one was open for 17% -> 20% of each run, Pallas kernels for 0% -> 0%
where the time goes in v4:
time: 341 us; the launch traced here: 340 us
  waiting for transfers between devices  147 us (43%)
  blocking collectives  67.7 us (20%)
  matrix products  48 us (14%)
  local copies, waits for them, and re-layouts  42.8 us (13%)
  between operations  14.1 us (4%)
  starting transfers between devices  10.4 us (3%)
  other arithmetic  9.7 us (3%)
    reduce_scatter x2, waiting for transfers between devices, local(): part = lax.psum_scatter(part, 'dp', scatter_dimension=0, tiled=False)  80.9 us
    all_to_all x2, blocking collectives, local(): lax.all_to_all(piece, 'expert', split_axis=0, concat_axis=0, tiled=True)  67.7 us
    all_gather x2, waiting for transfers between devices, local(): block = lax.all_gather(recv, 'dp', axis=0, tiled=True)  38 us
    all_to_all x1, waiting for transfers between devices, local(): lax.all_to_all(back, 'expert', split_axis=0, concat_axis=0, tiled=True)  28.2 us
    concatenate x5, local copies, waits for them, and re-layouts, local(): part = jnp.concatenate([token_part, gate_part[:, None], pad], axis=1)  17.4 us
    concatenate x3, local copies, waits for them, and re-layouts, dispatch(): return jnp.concatenate([slot_rows, slot_gates[:, None], pad], axis=1)  11.3 us
    all_to_all x1, starting transfers between devices, local(): lax.all_to_all(back, 'expert', split_axis=0, concat_axis=0, tiled=True)  10.1 us
    dot_general x2, matrix products, expert_one(): lax.dot_general(grad_upper, w_up, (((1,), (1,)), ((), ())), preferred_ele...  8.82 us
  transfers between devices with their start and end apart: 5, of which 5 were waited for; matrix products, arithmetic and copies ran while one was open for 20% of the time, Pallas kernels for 0%

profile of v4, /device:TPU:32, one launch (start us, length us, event | category | flops | bytes accessed | tf_op | source)
XLA Modules:
  0.0 339.8 jit_solution(2500592960619634818)
XLA Ops:
  10.4 1.5 convolution_convert_fusion
  11.9 1.6 concatenate.30
  13.6 9.4 %concatenate.32 = bf16[32,2,2,7296]{3,2,1,0:T(2,128)(2,1)S(1)} concatenate(bf16[32,2,2,7168]{3,2,1,0:T(2,128)(2,1)} %concatenate.30, bf16[32,2,2,1]{3,2,1,0:T(2,128)(2,1)S(1)} %concatenate.40, bf16[32,2,2,127]{3,2,1,0:T(2,128)(2,1)S(1)} %broadcast_in_dim.2), dimensions={3} | concatenate | bytes 3735552 | tf_op jit(solution)/shard_map/concatenate | solution.py:34
  23.1 1.3 slice_bitcast_fusion.1
  24.4 37.2 %all_to_all.29 = bf16[32,2,7296]{2,1,0:T(2,128)(2,1)S(1)} all-to-all(bf16[32,2,7296]{2,1,0:T(2,128)(2,1)S(1)} %get-tuple-element.6), channel_id=1, replica_groups=mesh['dp'=8,'expert'=32] {'expert'}, dimensions={0} | all-to-all | bytes 1867776 | tf_op jit(solution)/shard_map/all_to_all | solution.py:87
  61.5 1.3 all_to_all.24
  62.9 30.5 %all_to_all.30 = bf16[32,2,7296]{2,1,0:T(2,128)(2,1)S(1)} all-to-all(bf16[32,2,7296]{2,1,0:T(2,128)(2,1)S(1)} %get-tuple-element.5), channel_id=1, replica_groups=mesh['dp'=8,'expert'=32] {'expert'}, dimensions={0} | all-to-all | bytes 1867776 | tf_op jit(solution)/shard_map/all_to_all | solution.py:87
  94.8 13.1 %all-gather.5.cloned.1.call-done = bf16[512,7296]{1,0:T(8,128)(2,1)} async-done(((bf16[64,7296]{1,0:T(8,128)(2,1)}), bf16[512,7296]{1,0:T(8,128)(2,1)}) %all-gather.5.cloned.1.call-update) | async-done | bytes 7471120 | tf_op jit(solution)/shard_map/all_gather | solution.py:88
  108.9 3.5 %fusion.12 = f32[512,128]{1,0:T(8,128)S(1)} fusion(bf16[512,7296]{1,0:T(8,128)(2,1)} %all-gather.5.cloned.1.call-done, bf16[2,3584,128]{2,1,0:T(8,128)(2,1)} %param.11), kind=kOutput, calls=%fused_computation.26 | convolution fusion | flops 469762048 | bytes 4849664 | tf_op jit(solution)/shard_map/dot_general | solution.py:38
  112.5 3.3 fusion.25
  120.5 4.6 %convolution_add_fusion = f32[512,3584]{1,0:T(8,128)} fusion(f32[512,3584]{1,0:T(8,128)S(1)} %fusion.30, bf16[512,128]{1,0:T(8,128)(2,1)S(1)} %get-tuple-element.12, bf16[2,3584,128]{2,1,0:T(8,128)(2,1)S(1)} %copy-done.2), kind=kOutput, calls=%fused_computation.9 | convolution fusion | flops 471597056 | bytes 15728640 | tf_op jit(solution)/shard_map/dot_general | solution.py:56
  125.2 8.5 %concatenate.39 = f32[8,64,3712]{2,1,0:T(8,128)} concatenate(f32[8,64,3584]{2,1,0:T(8,128)} %bitcast.78, f32[8,64,1]{2,1,0:T(8,128)S(1)} %concatenate.42, f32[8,64,127]{2,1,0:T(8,128)S(1)} %concatenate.35), dimensions={2} | concatenate | bytes 15204352 | tf_op jit(solution)/shard_map/concatenate | solution.py:98
  133.9 24.9 %all-gather.3.cloned.1.call-done = bf16[512,7296]{1,0:T(8,128)(2,1)} async-done(((bf16[64,7296]{1,0:T(8,128)(2,1)}), bf16[512,7296]{1,0:T(8,128)(2,1)}) %all-gather.3.cloned.1.call-update) | async-done | bytes 7471120 | tf_op jit(solution)/shard_map/all_gather | solution.py:88
  160.0 3.3 fusion.18
  163.3 3.4 fusion.28
  170.9 4.2 %convolution_add_fusion.1 = f32[512,3584]{1,0:T(8,128)} fusion(f32[512,3584]{1,0:T(8,128)S(1)} %fusion.37, bf16[512,128]{1,0:T(8,128)(2,1)S(1)} %get-tuple-element.9, bf16[2,3584,128]{2,1,0:T(8,128)(2,1)S(1)} %copy-done.4), kind=kOutput, calls=%fused_computation.10 | convolution fusion | flops 471597056 | bytes 15728640 | tf_op jit(solution)/shard_map/dot_general | solution.py:56
  175.2 8.4 %concatenate.36 = f32[8,64,3712]{2,1,0:T(8,128)} concatenate(f32[8,64,3584]{2,1,0:T(8,128)} %bitcast.79, f32[8,64,1]{2,1,0:T(8,128)S(1)} %concatenate.41, f32[8,64,127]{2,1,0:T(8,128)S(1)} %concatenate.35), dimensions={2} | concatenate | bytes 15204352 | tf_op jit(solution)/shard_map/concatenate | solution.py:98
  183.6 29.2 %reduce-scatter.5.cloned.1.call-done = f32[1,64,3712]{2,1,0:T(8,128)} async-done(((f32[8,64,3712]{2,1,0:T(8,128)}), f32[1,64,3712]{2,1,0:T(8,128)}) %reduce-scatter.5.cloned.1.call-update) | async-done | bytes 950288 | tf_op jit(solution)/shard_map/reduce_scatter | solution.py:101
  212.8 1.7 stack_reshape_reduce_scatter.7
  214.6 51.6 %reduce-scatter.3.cloned.1.call-done = f32[1,64,3712]{2,1,0:T(8,128)} async-done(((f32[8,64,3712]{2,1,0:T(8,128)}), f32[1,64,3712]{2,1,0:T(8,128)}) %reduce-scatter.3.cloned.1.call-update) | async-done | bytes 950288 | tf_op jit(solution)/shard_map/reduce_scatter | solution.py:101
  266.2 1.7 stack_reshape_reduce_scatter.6
  268.0 2.2 pad_maximum_fusion
  270.2 10.1 %all-to-all-start.2 = ((f32[32,2,2,3712]{3,2,1,0:T(2,128)}), f32[32,2,2,3712]{3,2,1,0:T(2,128)S(1)}, u32[]{:S(2)}, u32[]{:S(2)}) async-start(f32[32,2,2,3712]{3,2,1,0:T(2,128)} %pad_maximum_fusion), calls=%async_computation.4 | async-start | bytes 3801088 | tf_op jit(solution)/shard_map/all_to_all | solution.py:107
  280.3 3.4 fusion.4
  283.7 3.4 fusion.6
  289.4 2.9 fusion.8
  293.3 1.4 pad_maximum_fusion.3
  294.7 1.4 pad_maximum_fusion.2
  296.1 1.4 pad_maximum_fusion.1
  297.5 28.2 %all-to-all-done.2 = f32[32,2,2,3712]{3,2,1,0:T(2,128)S(1)} async-done(((f32[32,2,2,3712]{3,2,1,0:T(2,128)}), f32[32,2,2,3712]{3,2,1,0:T(2,128)S(1)}, u32[]{:S(2)}, u32[]{:S(2)}) %all-to-all-start.2) | async-done | bytes 1900576 | tf_op jit(solution)/shard_map/all_to_all | solution.py:107
  325.7 2.6 reshape.83
  329.2 3.1 convolution_convert_fusion.7
  (68 shorter events, 21.3 us)
Async XLA Ops:
  7.2 100.7 %all-gather.5.cloned.1.call-start = ((), (), s32[]{:S(2)}) async-start(), calls=%async_computation.7 | async-start | bytes 8404992 | tf_op jit(solution)/shard_map/all_gather | solution.py:88
  62.8 96.0 %all-gather.3.cloned.1.call-start = ((), (), s32[]{:S(2)}) async-start(), calls=%async_computation.5 | async-start | bytes 8404992 | tf_op jit(solution)/shard_map/all_gather | solution.py:88
  94.7 17.7 %copy-start.5 = (bf16[2,128,3584]{2,1,0:T(8,128)(2,1)S(1)}, bf16[2,128,3584]{2,1,0:T(8,128)(2,1)}, u32[]{:S(2)}) copy-start(bf16[2,128,3584]{2,1,0:T(8,128)(2,1)} %param.13) | copy-start | bytes 5505028
  94.7 118.1 %reduce-scatter.5.cloned.1.call-start = ((), (), s32[]{:S(2)}) async-start(), calls=%async_computation.8 | async-start | bytes 8552448 | tf_op jit(solution)/shard_map/reduce_scatter | solution.py:101
  108.9 6.9 %slice-start = ((s8[7471104]{0:T(1024)(128)(4,1)}), s8[4194304]{0:T(1024)(128)(4,1)S(1)}, s32[]{:S(2)}) async-start(s8[7471104]{0:T(1024)(128)(4,1)} %bitcast.80), calls=%async_computation.9 | async-start | bytes 8388608
  112.4 3.4 copy-start.1
  112.5 3.6 %slice-start.1 = ((s8[7471104]{0:T(1024)(128)(4,1)}), s8[3276800]{0:T(1024)(128)(4,1)S(1)}, s32[]{:S(2)}) async-start(s8[7471104]{0:T(1024)(128)(4,1)} %bitcast.80), calls=%async_computation.10 | async-start | bytes 6553600
  116.0 1.5 copy-start.6
  117.5 1.5 copy-start
  119.0 1.5 copy-start.2
  133.7 132.6 %reduce-scatter.3.cloned.1.call-start = ((), (), s32[]{:S(2)}) async-start(), calls=%async_computation.6 | async-start | bytes 8552448 | tf_op jit(solution)/shard_map/reduce_scatter | solution.py:101
  158.8 4.5 %copy-start.7 = (bf16[2,128,3584]{2,1,0:T(8,128)(2,1)S(1)}, bf16[2,128,3584]{2,1,0:T(8,128)(2,1)}, u32[]{:S(2)}) copy-start(bf16[2,128,3584]{2,1,0:T(8,128)(2,1)} %param.13) | copy-start | bytes 5505028
  160.0 6.7 %slice-start.4 = ((s8[7471104]{0:T(1024)(128)(4,1)}), s8[4194304]{0:T(1024)(128)(4,1)S(1)}, s32[]{:S(2)}) async-start(s8[7471104]{0:T(1024)(128)(4,1)} %bitcast.84), calls=%async_computation.13 | async-start | bytes 8388608
  163.3 3.4 copy-start.3
  163.3 3.6 %slice-start.5 = ((s8[7471104]{0:T(1024)(128)(4,1)}), s8[3276800]{0:T(1024)(128)(4,1)S(1)}, s32[]{:S(2)}) async-start(s8[7471104]{0:T(1024)(128)(4,1)} %bitcast.84), calls=%async_computation.14 | async-start | bytes 6553600
  169.4 1.5 copy-start.4
  270.2 55.5 %all-to-all-start.2 = ((f32[32,2,2,3712]{3,2,1,0:T(2,128)}), f32[32,2,2,3712]{3,2,1,0:T(2,128)S(1)}, u32[]{:S(2)}, u32[]{:S(2)}) async-start(f32[32,2,2,3712]{3,2,1,0:T(2,128)} %pad_maximum_fusion), calls=%async_computation.4 | async-start | bytes 3801088 | tf_op jit(solution)/shard_map/all_to_all | solution.py:107
  280.3 6.8 %slice-start.2 = ((s8[7471104]{0:T(1024)(128)(4,1)}), s8[4194304]{0:T(1024)(128)(4,1)S(1)}, s32[]{:S(2)}) async-start(s8[7471104]{0:T(1024)(128)(4,1)} %bitcast.82), calls=%async_computation.11 | async-start | bytes 8388608
  283.6 3.4 slice-start.3
Sparse Core Ops, SparseCore 0:
  62.9 44.8 all-gather.4
  110.3 48.5 all-gather.2
  161.4 51.4 reduce-scatter.4
  215.3 50.9 reduce-scatter.2

commit v5 on v4

--- a/solution.py
+++ b/solution.py
@@ -98,8 +98,8 @@
         part = jnp.concatenate([token_part, gate_part[:, None], pad], axis=1)
         wide = part.shape[-1]
         part = part.reshape(n_groups, n_expert * capacity, wide)
-        part = lax.psum_scatter(part, "dp", scatter_dimension=0, tiled=False)
-        summed.append(part.reshape(n_expert, capacity, wide))
+        part = lax.psum_scatter(part.astype(jnp.bfloat16), "dp", scatter_dimension=0, tiled=False)
+        summed.append(part.astype(jnp.float32).reshape(n_expert, capacity, wide))
         grads_g.append(grad_g)
         grads_u.append(grad_u)
         grads_d.append(grad_d)

time: 341 us -> 316 us (0.927)
  waiting for transfers between devices: 147 us -> 128 us
  local copies, waits for them, and re-layouts: 42.8 us -> 38 us
    reduce_scatter x2, waiting for transfers between devices: 80.9 us -> 60.6 us  [local(): lax.psum_scatter(part.astype(jnp.bfloat16), 'dp', scatter_dimension=0, ti...]
    concatenate x5, local copies, waits for them, and re-layouts: 17.4 us -> 13.8 us  [local(): part = jnp.concatenate([token_part, gate_part[:, None], pad], axis=1)]
    another operation x2 -> x0, local copies, waits for them, and re-layouts: 3.5 us -> none  [local(): back = jnp.stack(summed, axis=1)]
    all_gather x2, waiting for transfers between devices: 38 us -> 41.5 us  [local(): block = lax.all_gather(recv, 'dp', axis=0, tiled=True)]
  transfers between devices with their start and end apart: 5 -> 5, of which waited for: 5 -> 5; matrix products, arithmetic and copies ran while one was open for 20% -> 19% of each run, Pallas kernels for 0% -> 0%
where the time goes in v5:
time: 316 us; the launch traced here: 313 us
  waiting for transfers between devices  128 us (41%)
  blocking collectives  67.7 us (21%)
  matrix products  45.2 us (14%)
  local copies, waits for them, and re-layouts  38 us (12%)
  between operations  14.1 us (4%)
  starting transfers between devices  10.4 us (3%)
  other arithmetic  9.78 us (3%)
    all_to_all x2, blocking collectives, local(): lax.all_to_all(piece, 'expert', split_axis=0, concat_axis=0, tiled=True)  67.7 us
    reduce_scatter x2, waiting for transfers between devices, local(): lax.psum_scatter(part.astype(jnp.bfloat16), 'dp', scatter_dimension=0, ti...  60.6 us
    all_gather x2, waiting for transfers between devices, local(): block = lax.all_gather(recv, 'dp', axis=0, tiled=True)  41.5 us
    all_to_all x1, waiting for transfers between devices, local(): lax.all_to_all(back, 'expert', split_axis=0, concat_axis=0, tiled=True)  25.9 us
    concatenate x5, local copies, waits for them, and re-layouts, local(): part = jnp.concatenate([token_part, gate_part[:, None], pad], axis=1)  13.8 us
    concatenate x3, local copies, waits for them, and re-layouts, dispatch(): return jnp.concatenate([slot_rows, slot_gates[:, None], pad], axis=1)  11.3 us
    all_to_all x1, starting transfers between devices, local(): lax.all_to_all(back, 'expert', split_axis=0, concat_axis=0, tiled=True)  10.1 us
    dot_general x2, matrix products, expert_one(): gate_pre = jnp.dot(rows_in, w_gate, preferred_element_type=jnp.float32)  6.83 us
  transfers between devices with their start and end apart: 5, of which 5 were waited for; matrix products, arithmetic and copies ran while one was open for 19% of the time, Pallas kernels for 0%

profile of v5, /device:TPU:32, one launch (start us, length us, event | category | flops | bytes accessed | tf_op | source)
XLA Modules:
  0.0 313.2 jit_solution(6801836065996059371)
XLA Ops:
  10.4 1.5 convolution_convert_fusion
  11.9 1.6 concatenate.32
  13.6 9.4 %concatenate.34 = bf16[32,2,2,7296]{3,2,1,0:T(2,128)(2,1)S(1)} concatenate(bf16[32,2,2,7168]{3,2,1,0:T(2,128)(2,1)} %concatenate.32, bf16[32,2,2,1]{3,2,1,0:T(2,128)(2,1)S(1)} %concatenate.42, bf16[32,2,2,127]{3,2,1,0:T(2,128)(2,1)S(1)} %broadcast_in_dim.2), dimensions={3} | concatenate | bytes 3735552 | tf_op jit(solution)/shard_map/concatenate | solution.py:34
  23.1 1.3 slice_bitcast_fusion.1
  24.4 37.2 %all_to_all.29 = bf16[32,2,7296]{2,1,0:T(2,128)(2,1)S(1)} all-to-all(bf16[32,2,7296]{2,1,0:T(2,128)(2,1)S(1)} %get-tuple-element.6), channel_id=1, replica_groups=mesh['dp'=8,'expert'=32] {'expert'}, dimensions={0} | all-to-all | bytes 1867776 | tf_op jit(solution)/shard_map/all_to_all | solution.py:87
  61.5 1.3 all_to_all.24
  62.9 30.5 %all_to_all.30 = bf16[32,2,7296]{2,1,0:T(2,128)(2,1)S(1)} all-to-all(bf16[32,2,7296]{2,1,0:T(2,128)(2,1)S(1)} %get-tuple-element.5), channel_id=1, replica_groups=mesh['dp'=8,'expert'=32] {'expert'}, dimensions={0} | all-to-all | bytes 1867776 | tf_op jit(solution)/shard_map/all_to_all | solution.py:87
  93.4 1.3 all_to_all.21
  94.8 13.1 %all-gather.5.cloned.1.call-done = bf16[512,7296]{1,0:T(8,128)(2,1)} async-done(((bf16[64,7296]{1,0:T(8,128)(2,1)}), bf16[512,7296]{1,0:T(8,128)(2,1)}) %all-gather.5.cloned.1.call-update) | async-done | bytes 7471120 | tf_op jit(solution)/shard_map/all_gather | solution.py:88
  108.9 3.5 %fusion.12 = f32[512,128]{1,0:T(8,128)S(1)} fusion(bf16[512,7296]{1,0:T(8,128)(2,1)} %all-gather.5.cloned.1.call-done, bf16[2,3584,128]{2,1,0:T(8,128)(2,1)} %param.11), kind=kOutput, calls=%fused_computation.26 | convolution fusion | flops 469762048 | bytes 4849664 | tf_op jit(solution)/shard_map/dot_general | solution.py:38
  112.5 3.3 %fusion.25 = f32[512,128]{1,0:T(8,128)S(1)} fusion(f32[512]{0:T(512)S(1)} %convert_reduce_fusion, bf16[512,7296]{1,0:T(8,128)(2,1)} %all-gather.5.cloned.1.call-done, bf16[2,128,3584]{2,1,0:T(8,128)(2,1)S(1)} %copy-done.5), kind=kOutput, calls=%fused_computation.42 | convolution fusion | flops 475267072 | bytes 4851712 | tf_op jit(solution)/shard_map/dot_general | solution.py:46
  120.5 3.0 add_convert_fusion
  123.5 6.6 %concatenate.41 = bf16[8,64,3712]{2,1,0:T(8,128)(2,1)} concatenate(bf16[8,64,3584]{2,1,0:T(8,128)(2,1)} %bitcast.78, bf16[8,64,1]{2,1,0:T(8,128)(2,1)S(1)} %concatenate.44, bf16[8,64,127]{2,1,0:T(8,128)(2,1)S(1)} %concatenate.37), dimensions={2} | concatenate | bytes 7602176 | tf_op jit(solution)/shard_map/concatenate | solution.py:98
  130.4 28.4 %all-gather.3.cloned.1.call-done = bf16[512,7296]{1,0:T(8,128)(2,1)} async-done(((bf16[64,7296]{1,0:T(8,128)(2,1)}), bf16[512,7296]{1,0:T(8,128)(2,1)}) %all-gather.3.cloned.1.call-update) | async-done | bytes 7471120 | tf_op jit(solution)/shard_map/all_gather | solution.py:88
  160.0 3.3 %fusion.18 = f32[512,128]{1,0:T(8,128)S(1)} fusion(bf16[512,7296]{1,0:T(8,128)(2,1)} %all-gather.3.cloned.1.call-done, bf16[2,3584,128]{2,1,0:T(8,128)(2,1)S(1)} %copy-done), kind=kOutput, calls=%fused_computation.32 | convolution fusion | flops 469762048 | bytes 4849664 | tf_op jit(solution)/shard_map/dot_general | solution.py:38
  163.3 3.4 %fusion.28 = f32[512,128]{1,0:T(8,128)S(1)} fusion(f32[512]{0:T(512)S(1)} %convert_reduce_fusion.1, bf16[512,7296]{1,0:T(8,128)(2,1)} %all-gather.3.cloned.1.call-done, bf16[2,128,3584]{2,1,0:T(8,128)(2,1)S(1)} %copy-done.7), kind=kOutput, calls=%fused_computation.43 | convolution fusion | flops 475267072 | bytes 4851712 | tf_op jit(solution)/shard_map/dot_general | solution.py:46
  168.0 1.2 fusion.1
  171.0 3.0 add_convert_fusion.1
  174.0 6.6 %concatenate.38 = bf16[8,64,3712]{2,1,0:T(8,128)(2,1)} concatenate(bf16[8,64,3584]{2,1,0:T(8,128)(2,1)} %bitcast.79, bf16[8,64,1]{2,1,0:T(8,128)(2,1)S(1)} %concatenate.43, bf16[8,64,127]{2,1,0:T(8,128)(2,1)S(1)} %concatenate.37), dimensions={2} | concatenate | bytes 7602176 | tf_op jit(solution)/shard_map/concatenate | solution.py:98
  180.6 20.7 %reduce-scatter.5.cloned.1.call-done = bf16[1,64,3712]{2,1,0:T(8,128)(2,1)} async-done(((bf16[8,64,3712]{2,1,0:T(8,128)(2,1)}), bf16[1,64,3712]{2,1,0:T(8,128)(2,1)}) %reduce-scatter.5.cloned.1.call-update) | async-done | bytes 475152 | tf_op jit(solution)/shard_map/reduce_scatter | solution.py:101
  202.5 39.9 %reduce-scatter.3.cloned.1.call-done = bf16[1,64,3712]{2,1,0:T(8,128)(2,1)} async-done(((bf16[8,64,3712]{2,1,0:T(8,128)(2,1)}), bf16[1,64,3712]{2,1,0:T(8,128)(2,1)}) %reduce-scatter.3.cloned.1.call-update) | async-done | bytes 475152 | tf_op jit(solution)/shard_map/reduce_scatter | solution.py:101
  243.6 2.3 maximum_convert_fusion
  245.9 10.1 %all-to-all-start.2 = ((f32[32,2,2,3712]{3,2,1,0:T(2,128)}), f32[32,2,2,3712]{3,2,1,0:T(2,128)S(1)}, u32[]{:S(2)}, u32[]{:S(2)}) async-start(f32[32,2,2,3712]{3,2,1,0:T(2,128)} %maximum_convert_fusion), calls=%async_computation.4 | async-start | bytes 3801088 | tf_op jit(solution)/shard_map/all_to_all | solution.py:107
  256.0 3.4 %fusion.4 = bf16[1,3584,128]{2,1,0:T(8,128)(2,1)S(1)} fusion(bf16[512,128]{1,0:T(8,128)(2,1)S(1)} %get-tuple-element.8, bf16[512,7296]{1,0:T(8,128)(2,1)} %all-gather.3.cloned.1.call-done), kind=kOutput, calls=%fused_computation.17 | convolution fusion | flops 470220800 | bytes 4718592 | tf_op jit(solution)/shard_map/dot_general | solution.py:59
  259.4 3.4 %fusion.6 = bf16[1,3584,128]{2,1,0:T(8,128)(2,1)S(1)} fusion(bf16[512,128]{1,0:T(8,128)(2,1)S(1)} %get-tuple-element.9, bf16[512,7296]{1,0:T(8,128)(2,1)} %all-gather.3.cloned.1.call-done), kind=kOutput, calls=%fused_computation.19 | convolution fusion | flops 470220800 | bytes 4718592 | tf_op jit(solution)/shard_map/dot_general | solution.py:62
  265.1 2.9 fusion.8
  269.0 1.4 pad_maximum_fusion.2
  270.4 1.4 pad_maximum_fusion.1
  271.8 1.4 pad_maximum_fusion
  273.2 25.9 %all-to-all-done.2 = f32[32,2,2,3712]{3,2,1,0:T(2,128)S(1)} async-done(((f32[32,2,2,3712]{3,2,1,0:T(2,128)}), f32[32,2,2,3712]{3,2,1,0:T(2,128)S(1)}, u32[]{:S(2)}, u32[]{:S(2)}) %all-to-all-start.2) | async-done | bytes 1900576 | tf_op jit(solution)/shard_map/all_to_all | solution.py:107
  299.1 2.6 reshape.111
  302.6 3.1 convolution_convert_fusion.7
  (68 shorter events, 21.2 us)
Async XLA Ops:
  7.2 100.7 %all-gather.5.cloned.1.call-start = ((), (), s32[]{:S(2)}) async-start(), calls=%async_computation.7 | async-start | bytes 8404992 | tf_op jit(solution)/shard_map/all_gather | solution.py:88
  62.8 96.0 %all-gather.3.cloned.1.call-start = ((), (), s32[]{:S(2)}) async-start(), calls=%async_computation.5 | async-start | bytes 8404992 | tf_op jit(solution)/shard_map/all_gather | solution.py:88
  94.7 17.7 %copy-start.5 = (bf16[2,128,3584]{2,1,0:T(8,128)(2,1)S(1)}, bf16[2,128,3584]{2,1,0:T(8,128)(2,1)}, u32[]{:S(2)}) copy-start(bf16[2,128,3584]{2,1,0:T(8,128)(2,1)} %param.13) | copy-start | bytes 5505028
  94.7 106.6 %reduce-scatter.5.cloned.1.call-start = ((), (), s32[]{:S(2)}) async-start(), calls=%async_computation.8 | async-start | bytes 4276224 | tf_op jit(solution)/shard_map/reduce_scatter | solution.py:101
  108.9 6.9 %slice-start = ((s8[7471104]{0:T(1024)(128)(4,1)}), s8[4194304]{0:T(1024)(128)(4,1)S(1)}, s32[]{:S(2)}) async-start(s8[7471104]{0:T(1024)(128)(4,1)} %bitcast.80), calls=%async_computation.9 | async-start | bytes 8388608
  112.4 3.4 %copy-start.1 = (bf16[2,3584,128]{2,1,0:T(8,128)(2,1)S(1)}, bf16[2,3584,128]{2,1,0:T(8,128)(2,1)}, u32[]{:S(2)}) copy-start(bf16[2,3584,128]{2,1,0:T(8,128)(2,1)} %param.12) | copy-start | bytes 5505028
  112.5 3.6 %slice-start.1 = ((s8[7471104]{0:T(1024)(128)(4,1)}), s8[3276800]{0:T(1024)(128)(4,1)S(1)}, s32[]{:S(2)}) async-start(s8[7471104]{0:T(1024)(128)(4,1)} %bitcast.80), calls=%async_computation.10 | async-start | bytes 6553600
  116.0 1.5 copy-start.6
  117.5 1.5 copy-start
  119.0 1.5 copy-start.2
  130.2 112.2 %reduce-scatter.3.cloned.1.call-start = ((), (), s32[]{:S(2)}) async-start(), calls=%async_computation.6 | async-start | bytes 4276224 | tf_op jit(solution)/shard_map/reduce_scatter | solution.py:101
  158.8 4.5 %copy-start.7 = (bf16[2,128,3584]{2,1,0:T(8,128)(2,1)S(1)}, bf16[2,128,3584]{2,1,0:T(8,128)(2,1)}, u32[]{:S(2)}) copy-start(bf16[2,128,3584]{2,1,0:T(8,128)(2,1)} %param.13) | copy-start | bytes 5505028
  160.0 6.7 %slice-start.4 = ((s8[7471104]{0:T(1024)(128)(4,1)}), s8[4194304]{0:T(1024)(128)(4,1)S(1)}, s32[]{:S(2)}) async-start(s8[7471104]{0:T(1024)(128)(4,1)} %bitcast.84), calls=%async_computation.13 | async-start | bytes 8388608
  163.3 3.4 %copy-start.3 = (bf16[2,3584,128]{2,1,0:T(8,128)(2,1)S(1)}, bf16[2,3584,128]{2,1,0:T(8,128)(2,1)}, u32[]{:S(2)}) copy-start(bf16[2,3584,128]{2,1,0:T(8,128)(2,1)} %param.12) | copy-start | bytes 5505028
  163.3 3.6 %slice-start.5 = ((s8[7471104]{0:T(1024)(128)(4,1)}), s8[3276800]{0:T(1024)(128)(4,1)S(1)}, s32[]{:S(2)}) async-start(s8[7471104]{0:T(1024)(128)(4,1)} %bitcast.84), calls=%async_computation.14 | async-start | bytes 6553600
  169.5 1.5 copy-start.4
  245.9 53.1 %all-to-all-start.2 = ((f32[32,2,2,3712]{3,2,1,0:T(2,128)}), f32[32,2,2,3712]{3,2,1,0:T(2,128)S(1)}, u32[]{:S(2)}, u32[]{:S(2)}) async-start(f32[32,2,2,3712]{3,2,1,0:T(2,128)} %maximum_convert_fusion), calls=%async_computation.4 | async-start | bytes 3801088 | tf_op jit(solution)/shard_map/all_to_all | solution.py:107
  256.0 6.8 %slice-start.2 = ((s8[7471104]{0:T(1024)(128)(4,1)}), s8[4194304]{0:T(1024)(128)(4,1)S(1)}, s32[]{:S(2)}) async-start(s8[7471104]{0:T(1024)(128)(4,1)} %bitcast.82), calls=%async_computation.11 | async-start | bytes 8388608
  259.4 3.4 %slice-start.3 = ((s8[7471104]{0:T(1024)(128)(4,1)}), s8[3276800]{0:T(1024)(128)(4,1)S(1)}, s32[]{:S(2)}) async-start(s8[7471104]{0:T(1024)(128)(4,1)} %bitcast.82), calls=%async_computation.12 | async-start | bytes 6553600
Sparse Core Ops, SparseCore 0:
  62.9 44.8 all-gather.4
  110.3 48.5 all-gather.2
  161.4 39.9 reduce-scatter.4
  203.7 38.6 reduce-scatter.2

commit v6 on v4

--- a/solution.py
+++ b/solution.py
@@ -99,12 +99,12 @@
         wide = part.shape[-1]
         part = part.reshape(n_groups, n_expert * capacity, wide)
         part = lax.psum_scatter(part, "dp", scatter_dimension=0, tiled=False)
-        summed.append(part.reshape(n_expert, capacity, wide))
+        part = part.reshape(n_expert, capacity, wide)
+        summed.append(lax.all_to_all(part, "expert", split_axis=0, concat_axis=0, tiled=True))
         grads_g.append(grad_g)
         grads_u.append(grad_u)
         grads_d.append(grad_d)
     back = jnp.stack(summed, axis=1)
-    back = lax.all_to_all(back, "expert", split_axis=0, concat_axis=0, tiled=True)
     back = back.reshape(slots, back.shape[-1])
     back_tokens = back[:, :width]
     back_gates = back[:, width]

time: 341 us -> 320 us (0.938)
  waiting for transfers between devices: 147 us -> 110 us
  starting transfers between devices: 10.4 us -> 20.4 us
  matrix products: 48 us -> 53 us
    reduce_scatter x2, waiting for transfers between devices: 80.9 us -> 53.1 us  [local(): part = lax.psum_scatter(part, 'dp', scatter_dimension=0, tiled=False)]
    all_to_all x1 -> x2, starting transfers between devices: 10.1 us -> 20.1 us  [local(): lax.all_to_all(part, 'expert', split_axis=0, concat_axis=0, tiled=True)]
    all_to_all x1 -> x2, waiting for transfers between devices: 28.2 us -> 18.4 us  [local(): lax.all_to_all(part, 'expert', split_axis=0, concat_axis=0, tiled=True)]
  transfers between devices with their start and end apart: 5 -> 6, of which waited for: 5 -> 5; matrix products, arithmetic and copies ran while one was open for 20% -> 24% of each run, Pallas kernels for 0% -> 0%
where the time goes in v6:
time: 320 us; the launch traced here: 319 us
  waiting for transfers between devices  110 us (34%)
  blocking collectives  67.7 us (21%)
  matrix products  53 us (17%)
  local copies, waits for them, and re-layouts  44.5 us (14%)
  starting transfers between devices  20.4 us (6%)
  between operations  14.1 us (4%)
  other arithmetic  9.7 us (3%)
    all_to_all x2, blocking collectives, local(): lax.all_to_all(piece, 'expert', split_axis=0, concat_axis=0, tiled=True)  67.7 us
    reduce_scatter x2, waiting for transfers between devices, local(): part = lax.psum_scatter(part, 'dp', scatter_dimension=0, tiled=False)  53.1 us
    all_gather x2, waiting for transfers between devices, local(): block = lax.all_gather(recv, 'dp', axis=0, tiled=True)  38 us
    all_to_all x2, starting transfers between devices, local(): lax.all_to_all(part, 'expert', split_axis=0, concat_axis=0, tiled=True)  20.1 us
    all_to_all x2, waiting for transfers between devices, local(): lax.all_to_all(part, 'expert', split_axis=0, concat_axis=0, tiled=True)  18.4 us
    concatenate x5, local copies, waits for them, and re-layouts, local(): part = jnp.concatenate([token_part, gate_part[:, None], pad], axis=1)  17.4 us
    concatenate x3, local copies, waits for them, and re-layouts, dispatch(): return jnp.concatenate([slot_rows, slot_gates[:, None], pad], axis=1)  11.3 us
    dot_general x2, matrix products, expert_one(): lax.dot_general(grad_upper, w_up, (((1,), (1,)), ((), ())), preferred_ele...  8.74 us
  transfers between devices with their start and end apart: 6, of which 5 were waited for; matrix products, arithmetic and copies ran while one was open for 24% of the time, Pallas kernels for 0%

profile of v6, /device:TPU:32, one launch (start us, length us, event | category | flops | bytes accessed | tf_op | source)
XLA Modules:
  0.0 319.0 jit_solution(17489685264401246126)
XLA Ops:
  10.4 1.5 convolution_convert_fusion
  11.9 1.6 concatenate.30
  13.6 9.4 %concatenate.32 = bf16[32,2,2,7296]{3,2,1,0:T(2,128)(2,1)S(1)} concatenate(bf16[32,2,2,7168]{3,2,1,0:T(2,128)(2,1)} %concatenate.30, bf16[32,2,2,1]{3,2,1,0:T(2,128)(2,1)S(1)} %concatenate.40, bf16[32,2,2,127]{3,2,1,0:T(2,128)(2,1)S(1)} %broadcast_in_dim.2), dimensions={3} | concatenate | bytes 3735552 | tf_op jit(solution)/shard_map/concatenate | solution.py:34
  24.4 37.2 %all_to_all.34 = bf16[32,2,7296]{2,1,0:T(2,128)(2,1)S(1)} all-to-all(bf16[32,2,7296]{2,1,0:T(2,128)(2,1)S(1)} %get-tuple-element.6), channel_id=1, replica_groups=mesh['dp'=8,'expert'=32] {'expert'}, dimensions={0} | all-to-all | bytes 1867776 | tf_op jit(solution)/shard_map/all_to_all | solution.py:87
  62.9 30.5 %all_to_all.35 = bf16[32,2,7296]{2,1,0:T(2,128)(2,1)S(1)} all-to-all(bf16[32,2,7296]{2,1,0:T(2,128)(2,1)S(1)} %get-tuple-element.5), channel_id=1, replica_groups=mesh['dp'=8,'expert'=32] {'expert'}, dimensions={0} | all-to-all | bytes 1867776 | tf_op jit(solution)/shard_map/all_to_all | solution.py:87
  94.8 13.1 %all-gather.5.cloned.1.call-done = bf16[512,7296]{1,0:T(8,128)(2,1)} async-done(((bf16[64,7296]{1,0:T(8,128)(2,1)}), bf16[512,7296]{1,0:T(8,128)(2,1)}) %all-gather.5.cloned.1.call-update) | async-done | bytes 7471120 | tf_op jit(solution)/shard_map/all_gather | solution.py:88
  108.9 3.5 %fusion.12 = f32[512,128]{1,0:T(8,128)S(1)} fusion(bf16[512,7296]{1,0:T(8,128)(2,1)} %all-gather.5.cloned.1.call-done, bf16[2,3584,128]{2,1,0:T(8,128)(2,1)} %param.11), kind=kOutput, calls=%fused_computation.26 | convolution fusion | flops 469762048 | bytes 4849664 | tf_op jit(solution)/shard_map/dot_general | solution.py:38
  112.5 3.3 %fusion.25 = f32[512,128]{1,0:T(8,128)S(1)} fusion(f32[512]{0:T(512)S(1)} %convert_reduce_fusion, bf16[512,7296]{1,0:T(8,128)(2,1)} %all-gather.5.cloned.1.call-done, bf16[2,128,3584]{2,1,0:T(8,128)(2,1)S(1)} %copy-done.9), kind=kOutput, calls=%fused_computation.43 | convolution fusion | flops 475267072 | bytes 4851712 | tf_op jit(solution)/shard_map/dot_general | solution.py:46
  120.5 4.6 %convolution_add_fusion = f32[512,3584]{1,0:T(8,128)} fusion(f32[512,3584]{1,0:T(8,128)S(1)} %fusion.30, bf16[512,128]{1,0:T(8,128)(2,1)S(1)} %get-tuple-element.12, bf16[2,3584,128]{2,1,0:T(8,128)(2,1)S(1)} %copy-done.2), kind=kOutput, calls=%fused_computation.9 | convolution fusion | flops 471597056 | bytes 15728640 | tf_op jit(solution)/shard_map/dot_general | solution.py:56
  125.2 8.5 %concatenate.39 = f32[8,64,3712]{2,1,0:T(8,128)} concatenate(f32[8,64,3584]{2,1,0:T(8,128)} %bitcast.80, f32[8,64,1]{2,1,0:T(8,128)S(1)} %concatenate.42, f32[8,64,127]{2,1,0:T(8,128)S(1)} %concatenate.35), dimensions={2} | concatenate | bytes 15204352 | tf_op jit(solution)/shard_map/concatenate | solution.py:98
  133.9 24.9 %all-gather.3.cloned.1.call-done = bf16[512,7296]{1,0:T(8,128)(2,1)} async-done(((bf16[64,7296]{1,0:T(8,128)(2,1)}), bf16[512,7296]{1,0:T(8,128)(2,1)}) %all-gather.3.cloned.1.call-update) | async-done | bytes 7471120 | tf_op jit(solution)/shard_map/all_gather | solution.py:88
  160.0 3.3 %fusion.18 = f32[512,128]{1,0:T(8,128)S(1)} fusion(bf16[512,7296]{1,0:T(8,128)(2,1)} %all-gather.3.cloned.1.call-done, bf16[2,3584,128]{2,1,0:T(8,128)(2,1)S(1)} %copy-done), kind=kOutput, calls=%fused_computation.32 | convolution fusion | flops 469762048 | bytes 4849664 | tf_op jit(solution)/shard_map/dot_general | solution.py:38
  163.3 3.4 %fusion.28 = f32[512,128]{1,0:T(8,128)S(1)} fusion(f32[512]{0:T(512)S(1)} %convert_reduce_fusion.1, bf16[512,7296]{1,0:T(8,128)(2,1)} %all-gather.3.cloned.1.call-done, bf16[2,128,3584]{2,1,0:T(8,128)(2,1)S(1)} %copy-done.11), kind=kOutput, calls=%fused_computation.44 | convolution fusion | flops 475267072 | bytes 4851712 | tf_op jit(solution)/shard_map/dot_general | solution.py:46
  171.6 4.1 %convolution_add_fusion.1 = f32[512,3584]{1,0:T(8,128)} fusion(f32[512,3584]{1,0:T(8,128)S(1)} %fusion.37, bf16[512,128]{1,0:T(8,128)(2,1)S(1)} %get-tuple-element.9, bf16[2,3584,128]{2,1,0:T(8,128)(2,1)S(1)} %copy-done.4), kind=kOutput, calls=%fused_computation.10 | convolution fusion | flops 471597056 | bytes 15728640 | tf_op jit(solution)/shard_map/dot_general | solution.py:56
  175.7 8.5 %concatenate.36 = f32[8,64,3712]{2,1,0:T(8,128)} concatenate(f32[8,64,3584]{2,1,0:T(8,128)} %bitcast.81, f32[8,64,1]{2,1,0:T(8,128)S(1)} %concatenate.41, f32[8,64,127]{2,1,0:T(8,128)S(1)} %concatenate.35), dimensions={2} | concatenate | bytes 15204352 | tf_op jit(solution)/shard_map/concatenate | solution.py:98
  184.2 28.7 %reduce-scatter.5.cloned.1.call-done = f32[1,64,3712]{2,1,0:T(8,128)} async-done(((f32[8,64,3712]{2,1,0:T(8,128)}), f32[1,64,3712]{2,1,0:T(8,128)}) %reduce-scatter.5.cloned.1.call-update) | async-done | bytes 950288 | tf_op jit(solution)/shard_map/reduce_scatter | solution.py:101
  212.9 2.7 reshape_reduce_scatter.7
  215.6 10.0 %all-to-all-start.3 = ((f32[32,2,3712]{2,1,0:T(2,128)}), f32[32,2,3712]{2,1,0:T(2,128)S(1)}, u32[]{:S(2)}, u32[]{:S(2)}) async-start(f32[32,2,3712]{2,1,0:T(2,128)} %reshape_reduce_scatter.7), calls=%async_computation.5 | async-start | bytes 1900544 | tf_op jit(solution)/shard_map/all_to_all | solution.py:103
  225.6 3.8 %fusion.4 = bf16[1,3584,128]{2,1,0:T(8,128)(2,1)S(1)} fusion(bf16[512,128]{1,0:T(8,128)(2,1)S(1)} %get-tuple-element.8, bf16[512,7296]{1,0:T(8,128)(2,1)} %all-gather.3.cloned.1.call-done), kind=kOutput, calls=%fused_computation.17 | convolution fusion | flops 470220800 | bytes 4718592 | tf_op jit(solution)/shard_map/dot_general | solution.py:59
  229.4 4.3 %fusion.6 = bf16[1,3584,128]{2,1,0:T(8,128)(2,1)} fusion(bf16[512,128]{1,0:T(8,128)(2,1)S(1)} %get-tuple-element.9, bf16[512,7296]{1,0:T(8,128)(2,1)} %all-gather.3.cloned.1.call-done), kind=kOutput, calls=%fused_computation.19 | convolution fusion | flops 470220800 | bytes 4718592 | tf_op jit(solution)/shard_map/dot_general | solution.py:62
  233.7 2.1 fusion.5
  235.9 4.1 %fusion.8 = bf16[1,128,3584]{2,1,0:T(8,128)(2,1)} fusion(bf16[512,128]{1,0:T(8,128)(2,1)S(1)} %copy-done.13, f32[512]{0:T(512)S(1)} %convert_reduce_fusion.1, bf16[512,7296]{1,0:T(8,128)(2,1)} %all-gather.3.cloned.1.call-done), kind=kOutput, calls=%fused_computation.21 | convolution fusion | flops 475725824 | bytes 4720640 | tf_op jit(solution)/shard_map/dot_general | solution.py:65
  239.9 1.9 fusion.9
  241.8 24.4 %reduce-scatter.3.cloned.1.call-done = f32[1,64,3712]{2,1,0:T(8,128)} async-done(((f32[8,64,3712]{2,1,0:T(8,128)}), f32[1,64,3712]{2,1,0:T(8,128)}) %reduce-scatter.3.cloned.1.call-update) | async-done | bytes 950288 | tf_op jit(solution)/shard_map/reduce_scatter | solution.py:101
  266.2 2.7 reshape_reduce_scatter.6
  268.9 10.1 %all-to-all-start.1 = ((f32[32,2,3712]{2,1,0:T(2,128)}), f32[32,2,3712]{2,1,0:T(2,128)S(1)}, u32[]{:S(2)}, u32[]{:S(2)}) async-start(f32[32,2,3712]{2,1,0:T(2,128)} %reshape_reduce_scatter.6), calls=%async_computation.2 | async-start | bytes 1900544 | tf_op jit(solution)/shard_map/all_to_all | solution.py:103
  279.0 3.3 %fusion.7 = bf16[1,3584,128]{2,1,0:T(8,128)(2,1)S(1)} fusion(bf16[512,128]{1,0:T(8,128)(2,1)S(1)} %get-tuple-element.12, bf16[512,7296]{1,0:T(8,128)(2,1)} %all-gather.5.cloned.1.call-done), kind=kOutput, calls=%fused_computation.20 | convolution fusion | flops 470220800 | bytes 4718592 | tf_op jit(solution)/shard_map/dot_general | solution.py:62
  282.4 1.4 pad_maximum_fusion.3
  286.6 18.4 %all-to-all-done.1 = f32[32,2,3712]{2,1,0:T(2,128)S(1)} async-done(((f32[32,2,3712]{2,1,0:T(2,128)}), f32[32,2,3712]{2,1,0:T(2,128)S(1)}, u32[]{:S(2)}, u32[]{:S(2)}) %all-to-all-start.1) | async-done | bytes 950304 | tf_op jit(solution)/shard_map/all_to_all | solution.py:103
  304.9 2.2 pad_maximum_fusion
  307.2 2.6 reshape.83
  309.9 1.6 convolution_convert_fusion.7
  (82 shorter events, 23.1 us)
Async XLA Ops:
  7.2 100.7 %all-gather.5.cloned.1.call-start = ((), (), s32[]{:S(2)}) async-start(), calls=%async_computation.8 | async-start | bytes 8404992 | tf_op jit(solution)/shard_map/all_gather | solution.py:88
  62.8 96.0 %all-gather.3.cloned.1.call-start = ((), (), s32[]{:S(2)}) async-start(), calls=%async_computation.6 | async-start | bytes 8404992 | tf_op jit(solution)/shard_map/all_gather | solution.py:88
  94.7 17.7 %copy-start.9 = (bf16[2,128,3584]{2,1,0:T(8,128)(2,1)S(1)}, bf16[2,128,3584]{2,1,0:T(8,128)(2,1)}, u32[]{:S(2)}) copy-start(bf16[2,128,3584]{2,1,0:T(8,128)(2,1)} %param.13) | copy-start | bytes 5505028
  94.7 118.2 %reduce-scatter.5.cloned.1.call-start = ((), (), s32[]{:S(2)}) async-start(), calls=%async_computation.9 | async-start | bytes 8552448 | tf_op jit(solution)/shard_map/reduce_scatter | solution.py:101
  108.9 6.9 %slice-start = ((s8[7471104]{0:T(1024)(128)(4,1)}), s8[4194304]{0:T(1024)(128)(4,1)S(1)}, s32[]{:S(2)}) async-start(s8[7471104]{0:T(1024)(128)(4,1)} %bitcast.84), calls=%async_computation.10 | async-start | bytes 8388608
  112.4 3.4 %copy-start.1 = (bf16[2,3584,128]{2,1,0:T(8,128)(2,1)S(1)}, bf16[2,3584,128]{2,1,0:T(8,128)(2,1)}, u32[]{:S(2)}) copy-start(bf16[2,3584,128]{2,1,0:T(8,128)(2,1)} %param.12) | copy-start | bytes 5505028
  112.5 3.6 %slice-start.1 = ((s8[7471104]{0:T(1024)(128)(4,1)}), s8[3276800]{0:T(1024)(128)(4,1)S(1)}, s32[]{:S(2)}) async-start(s8[7471104]{0:T(1024)(128)(4,1)} %bitcast.84), calls=%async_computation.11 | async-start | bytes 6553600
  116.0 1.5 copy-start.10
  117.5 1.5 copy-start
  119.0 1.5 copy-start.2
  133.6 132.6 %reduce-scatter.3.cloned.1.call-start = ((), (), s32[]{:S(2)}) async-start(), calls=%async_computation.7 | async-start | bytes 8552448 | tf_op jit(solution)/shard_map/reduce_scatter | solution.py:101
  158.8 4.5 %copy-start.11 = (bf16[2,128,3584]{2,1,0:T(8,128)(2,1)S(1)}, bf16[2,128,3584]{2,1,0:T(8,128)(2,1)}, u32[]{:S(2)}) copy-start(bf16[2,128,3584]{2,1,0:T(8,128)(2,1)} %param.13) | copy-start | bytes 5505028
  160.0 6.7 %slice-start.4 = ((s8[7471104]{0:T(1024)(128)(4,1)}), s8[4194304]{0:T(1024)(128)(4,1)S(1)}, s32[]{:S(2)}) async-start(s8[7471104]{0:T(1024)(128)(4,1)} %bitcast.88), calls=%async_computation.14 | async-start | bytes 8388608
  163.3 3.4 %copy-start.3 = (bf16[2,3584,128]{2,1,0:T(8,128)(2,1)S(1)}, bf16[2,3584,128]{2,1,0:T(8,128)(2,1)}, u32[]{:S(2)}) copy-start(bf16[2,3584,128]{2,1,0:T(8,128)(2,1)} %param.12) | copy-start | bytes 5505028
  163.3 3.6 %slice-start.5 = ((s8[7471104]{0:T(1024)(128)(4,1)}), s8[3276800]{0:T(1024)(128)(4,1)S(1)}, s32[]{:S(2)}) async-start(s8[7471104]{0:T(1024)(128)(4,1)} %bitcast.88), calls=%async_computation.15 | async-start | bytes 6553600
  168.0 0.7 copy-start.12
  170.1 1.5 copy-start.4
  215.6 53.4 %all-to-all-start.3 = ((f32[32,2,3712]{2,1,0:T(2,128)}), f32[32,2,3712]{2,1,0:T(2,128)S(1)}, u32[]{:S(2)}, u32[]{:S(2)}) async-start(f32[32,2,3712]{2,1,0:T(2,128)} %reshape_reduce_scatter.7), calls=%async_computation.5 | async-start | bytes 1900544 | tf_op jit(solution)/shard_map/all_to_all | solution.py:103
  225.6 8.1 %slice-start.2 = ((s8[7471104]{0:T(1024)(128)(4,1)}), s8[4194304]{0:T(1024)(128)(4,1)S(1)}, s32[]{:S(2)}) async-start(s8[7471104]{0:T(1024)(128)(4,1)} %bitcast.86), calls=%async_computation.12 | async-start | bytes 8388608
  229.4 4.3 %slice-start.3 = ((s8[7471104]{0:T(1024)(128)(4,1)}), s8[3276800]{0:T(1024)(128)(4,1)S(1)}, s32[]{:S(2)}) async-start(s8[7471104]{0:T(1024)(128)(4,1)} %bitcast.86), calls=%async_computation.13 | async-start | bytes 6553600
  233.7 2.1 copy-start.13
  268.9 36.0 %all-to-all-start.1 = ((f32[32,2,3712]{2,1,0:T(2,128)}), f32[32,2,3712]{2,1,0:T(2,128)S(1)}, u32[]{:S(2)}, u32[]{:S(2)}) async-start(f32[32,2,3712]{2,1,0:T(2,128)} %reshape_reduce_scatter.6), calls=%async_computation.2 | async-start | bytes 1900544 | tf_op jit(solution)/shard_map/all_to_all | solution.py:103
  279.0 3.4 %copy-start.7 = (bf16[1,128,3584]{2,1,0:T(8,128)(2,1)S(1)}, bf16[1,128,3584]{2,1,0:T(8,128)(2,1)}, u32[]{:S(2)}) copy-start(bf16[1,128,3584]{2,1,0:T(8,128)(2,1)} %fusion.8) | copy-start | bytes 2752516
  279.0 3.4 %copy-start.8 = (bf16[1,128,3584]{2,1,0:T(8,128)(2,1)S(1)}, bf16[1,128,3584]{2,1,0:T(8,128)(2,1)}, u32[]{:S(2)}) copy-start(bf16[1,128,3584]{2,1,0:T(8,128)(2,1)} %fusion.9) | copy-start | bytes 2752516
  282.4 1.4 copy-start.6
  282.4 2.8 copy-start.5
Sparse Core Ops, SparseCore 0:
  62.9 44.8 all-gather.4
  110.3 48.5 all-gather.2
  161.4 51.4 reduce-scatter.4
  215.3 50.8 reduce-scatter.2
